TPU v7x, 128 devices: a whole 4x4x4 slice. The times are simulated.
128 devices in a mesh: req: 32 (over x, z, core), tp: 4 (over y).
Axes of the slice: x: 4, y: 4, z: 4, core: 2. Of those that a mesh axis runs over, the one named last changes fastest.
Arguments:
- hidden_states: bfloat16 [8192, 2048], P('req'), may hold values from -30 to 30
- norm_gain: float32 [2048], replicated, may hold values from 0.5 to 1.5
- head: bfloat16 [2048, 98304], P(None, ('req', 'tp')), may hold values from -1 to 1
- target_ids: int32 [8192], P('req'), may hold values from 0 to 98303
- lengths: int32 [32], P('req'), may hold values from 32 to 256, as said below
Outputs:
- token_logprob: float32 [8192], P('req')
- token_entropy: float32 [8192], P('req')
- seq_mean_logprob: float32 [32], P('req')
- seq_top_logit: float32 [32], P('req')
Inputs may be any that keep to these rules, and one draw needn't show every extreme that they name: `lengths`: each completion has at least 32 and at most 256 live slots; some completion has exactly 256.
All inputs are finite; a program needn't handle non-finite values.
Results may differ from a plain program's by a relative error of at most 0.0018.
Values may be sent and summed in bfloat16 or wider, within the bound.
A program may use at most 128 MiB of HBM per device.

v0:
```python
import jax
import jax.numpy as jnp
import numpy as np
from jax import lax
from jax.experimental import pallas as pl
from jax.experimental.pallas import tpu as pltpu
from jax.sharding import Mesh, PartitionSpec as P

MESH = pl.DeviceIdType.MESH
EXTRA = 128


def swap_kernel(src_ref, dst_ref, send_sem, recv_sem):
    peer = (lax.axis_index("x"), lax.axis_index("z"), 1 - lax.axis_index("core"), lax.axis_index("tp"))
    barrier = pltpu.get_barrier_semaphore()
    pl.semaphore_signal(barrier, inc=1, device_id=peer, device_id_type=MESH)
    pl.semaphore_wait(barrier, 1)
    copy = pltpu.make_async_remote_copy(
        src_ref=src_ref,
        dst_ref=dst_ref,
        send_sem=send_sem,
        recv_sem=recv_sem,
        device_id=peer,
        device_id_type=MESH,
    )
    copy.start()
    copy.wait()


def swap_with_other_core(head):
    return pl.pallas_call(
        swap_kernel,
        out_shape=jax.ShapeDtypeStruct(head.shape, head.dtype),
        in_specs=[pl.BlockSpec(memory_space=pl.ANY)],
        out_specs=pl.BlockSpec(memory_space=pl.ANY),
        scratch_shapes=[pltpu.SemaphoreType.DMA, pltpu.SemaphoreType.DMA],
        compiler_params=pltpu.CompilerParams(collective_id=0, has_side_effects=True),
    )(head)


def slice_stats(block, target, matrix, vocab_ids):
    logits = jnp.dot(block, matrix, preferred_element_type=jnp.float32)
    top = jnp.max(logits, axis=-1)
    shifted = jnp.exp(logits - top[:, None])
    weight_sum = jnp.sum(shifted, axis=-1)
    weighted = jnp.sum(shifted * logits, axis=-1)
    hit = vocab_ids == target[:, None]
    picked = jnp.sum(jnp.where(hit, logits, 0.0), axis=-1)
    return jnp.stack([top, weight_sum, weighted, picked])


def merge(stats, axis):
    top = jnp.max(stats[:, 0], axis=axis)
    factor = jnp.exp(stats[:, 0] - jnp.expand_dims(top, axis))
    return (
        top,
        jnp.sum(stats[:, 1] * factor, axis=axis),
        jnp.sum(stats[:, 2] * factor, axis=axis),
        jnp.sum(stats[:, 3], axis=axis),
    )


def gather_kernel(piece_ref, out_ref, own_sem, send_sems, recv_sems):
    xi, zi = lax.axis_index("x"), lax.axis_index("z")
    core, tp = lax.axis_index("core"), lax.axis_index("tp")

    def dev(dx, dz):
        return (lax.rem(xi + dx, 4), lax.rem(zi + dz, 4), core, tp)

    barrier = pltpu.get_barrier_semaphore()
    for dx, dz in ((1, 0), (3, 0), (0, 1), (0, 3)):
        pl.semaphore_signal(barrier, inc=1, device_id=dev(dx, dz), device_id_type=MESH)
    pl.semaphore_wait(barrier, 4)
    own = pltpu.make_async_copy(piece_ref, out_ref.at[0, 0], own_sem)
    own.start()
    rows = piece_ref.shape[0]
    h, q = rows // 2, rows // 4
    count = [0]

    def send(src, dst, dx, dz):
        k = count[0]
        count[0] += 1
        cp = pltpu.make_async_remote_copy(
            src_ref=src,
            dst_ref=dst,
            send_sem=send_sems.at[k],
            recv_sem=recv_sems.at[k],
            device_id=dev(dx, dz),
            device_id_type=MESH,
        )
        cp.start()
        return cp

    def finish(cps):
        for cp in cps:
            cp.wait()

    finish([
        send(piece_ref.at[0:h], out_ref.at[0, 3, 0:h], 1, 0),
        send(piece_ref.at[0:h], out_ref.at[0, 1, 0:h], 3, 0),
        send(piece_ref.at[h:rows], out_ref.at[3, 0, h:rows], 0, 1),
        send(piece_ref.at[h:rows], out_ref.at[1, 0, h:rows], 0, 3),
    ])
    finish([
        send(out_ref.at[0, 3, 0:q], out_ref.at[0, 2, 0:q], 1, 0),
        send(out_ref.at[0, 1, q:h], out_ref.at[0, 2, q:h], 3, 0),
        send(out_ref.at[3, 0, h:h + q], out_ref.at[2, 0, h:h + q], 0, 1),
        send(out_ref.at[1, 0, h + q:rows], out_ref.at[2, 0, h + q:rows], 0, 3),
    ])
    own.wait()
    finish([
        send(out_ref.at[0, :, 0:h], out_ref.at[3, :, 0:h], 0, 1),
        send(out_ref.at[0, :, 0:h], out_ref.at[1, :, 0:h], 0, 3),
        send(out_ref.at[:, 0, h:rows], out_ref.at[:, 3, h:rows], 1, 0),
        send(out_ref.at[:, 0, h:rows], out_ref.at[:, 1, h:rows], 3, 0),
    ])
    finish([
        send(out_ref.at[3, :, 0:q], out_ref.at[2, :, 0:q], 0, 1),
        send(out_ref.at[1, :, q:h], out_ref.at[2, :, q:h], 0, 3),
        send(out_ref.at[:, 3, h:h + q], out_ref.at[:, 2, h:h + q], 1, 0),
        send(out_ref.at[:, 1, h + q:rows], out_ref.at[:, 2, h + q:rows], 3, 0),
    ])


def gather_plane(piece):
    rows, cols = piece.shape
    return pl.pallas_call(
        gather_kernel,
        out_shape=jax.ShapeDtypeStruct((4, 4, rows, cols), piece.dtype),
        in_specs=[pl.BlockSpec(memory_space=pl.ANY)],
        out_specs=pl.BlockSpec(memory_space=pl.ANY),
        scratch_shapes=[
            pltpu.SemaphoreType.DMA,
            pltpu.SemaphoreType.DMA((16,)),
            pltpu.SemaphoreType.DMA((16,)),
        ],
        compiler_params=pltpu.CompilerParams(collective_id=1, has_side_effects=True),
    )(piece)


def per_device(hidden_states, norm_gain, head, target_ids, lengths):
    feats = hidden_states.astype(jnp.float32)
    scale = lax.rsqrt(jnp.mean(feats * feats, axis=-1, keepdims=True) + 1e-06)
    normed = (feats * scale * norm_gain).astype(jnp.bfloat16)
    rows, dim = normed.shape
    vdev = head.shape[1]
    n_tp = lax.axis_size("tp")
    xi = lax.axis_index("x")
    zi = lax.axis_index("z")
    core = lax.axis_index("core")
    tp = lax.axis_index("tp")
    n_z = lax.axis_size("z")
    chip = xi * n_z + zi
    digits = jnp.stack([target_ids % 64, (target_ids // 64) % 64, target_ids // 4096], axis=1)
    tail = jnp.zeros((rows, EXTRA), jnp.bfloat16).at[:, :3].set(digits.astype(jnp.bfloat16))
    piece = jnp.concatenate([normed, tail], axis=1)
    head_ext = jnp.concatenate([head, jnp.zeros((EXTRA, vdev), head.dtype)], axis=0)
    other_head = swap_with_other_core(head_ext)
    columns = lax.broadcasted_iota(jnp.int32, (1, vdev), 1)
    own_ids = columns + ((chip * 2 + core) * n_tp + tp) * vdev
    other_ids = columns + ((chip * 2 + 1 - core) * n_tp + tp) * vdev

    def stats_of(block):
        lead = block.shape[:-2]
        flat = block.reshape(-1, block.shape[-1])
        code = flat[:, dim:dim + 3].astype(jnp.int32)
        target = code[:, 0] + code[:, 1] * 64 + code[:, 2] * 4096
        s_own = slice_stats(flat, target, head_ext, own_ids)
        s_other = slice_stats(flat, target, other_head, other_ids)
        first = jnp.where(core == 0, s_own, s_other)
        second = jnp.where(core == 0, s_other, s_own)
        merged = jnp.stack(merge(jnp.stack([first, second]), axis=0))
        return merged.reshape(4, *lead, block.shape[-2])

    gathered = gather_plane(piece)
    rel = stats_of(gathered.reshape(-1, gathered.shape[-1])).reshape(4, 4, 4, rows)
    absolute = jnp.roll(jnp.roll(rel, zi, axis=1), xi, axis=2)
    by_chip = jnp.swapaxes(absolute, 1, 2).reshape(4, -1, rows)
    arrived = lax.all_to_all(by_chip, ("x", "z"), split_axis=1, concat_axis=1, tiled=True)
    own = jnp.stack(merge(jnp.moveaxis(arrived, 1, 0), axis=0))
    everyone = lax.all_gather(own, "tp", axis=0)
    top, weight_sum, weighted, picked = merge(everyone, axis=0)
    log_norm = top + jnp.log(weight_sum)
    live = jnp.arange(rows, dtype=jnp.int32) < lengths[0]
    logprob = jnp.where(live, picked - log_norm, jnp.float32(0.0))
    entropy = jnp.where(live, log_norm - weighted / weight_sum, jnp.float32(0.0))
    mean_lp = (jnp.sum(logprob) / lengths[0].astype(jnp.float32)).reshape(1)
    top_live = jnp.max(jnp.where(live, top, jnp.float32(-1e30))).reshape(1)
    return (logprob, entropy, mean_lp, top_live)


def solution(mesh):
    n_req, n_tp = mesh.devices.shape
    devices = np.asarray(mesh.devices).reshape(4, n_req // 8, 2, n_tp)
    fine = Mesh(devices, ("x", "z", "core", "tp"))
    rq = ("x", "z", "core")
    in_specs = (P(rq, None), P(), P(None, (*rq, "tp")), P(rq), P(rq))
    out_specs = (P(rq), P(rq), P(rq), P(rq))
    return jax.shard_map(
        per_device, mesh=fine, in_specs=in_specs, out_specs=out_specs, check_vma=False
    )
```

profile of v0, /device:TPU:0, one launch (start us, length us, event | category | flops | bytes accessed | tf_op | source)
XLA Modules:
  0.0 213.6 jit_solution(1084791182539018257)
XLA Ops:
  0.6 0.6 compare_reduce_fusion
  1.3 1.5 fusion.3
  2.8 0.7 fusion.36
  3.5 0.1 copy.43
  3.7 0.7 broadcast_select_fusion.2
  4.4 1.5 fusion.5
  5.9 1.1 fusion.6.piece_ref
  7.0 115.3 %shard_map.84 = bf16[4,4,256,2176]{3,2,1,0:T(8,128)(2,1)} custom-call(bf16[256,2176]{1,0:T(8,128)(2,1)} %fusion.6.piece_ref), custom_call_target="tpu_custom_call" | custom-call | tf_op jit(solution)/shard_map/pallas_call | solution.py:127
  122.4 1.3 slice.83
  123.7 20.6 %fusion.46 = (f32[4096]{0:T(1024)S(1)}, f32[4096,768]{0,1:T(8,128)}) fusion(bf16[4096,2176]{1,0:T(8,128)(2,1)} %bitcast.85, bf16[2048,768]{1,0:T(8,128)(2,1)} %param.9), kind=kOutput, calls=%fused_computation.116 | convolution fusion | flops 13693349888 | bytes 33570816 | tf_op jit(solution)/shard_map/dot_general | solution.py:42
  144.3 1.9 concatenate.46.src_ref
  146.2 6.3 %shard_map.85 = bf16[2176,768]{1,0:T(8,128)(2,1)} custom-call(bf16[2176,768]{1,0:T(8,128)(2,1)} %concatenate.46.src_ref), custom_call_target="tpu_custom_call" | custom-call | tf_op jit(solution)/shard_map/pallas_call | solution.py:31
  152.5 0.4 copy.52
  153.0 20.7 %fusion.47 = (f32[4096]{0:T(1024)S(1)}, f32[4096,768]{0,1:T(8,128)}) fusion(bf16[4096,2176]{1,0:T(8,128)(2,1)} %bitcast.86, bf16[2176,768]{1,0:T(8,128)(2,1)} %shard_map.85), kind=kOutput, calls=%fused_computation.117 | convolution fusion | flops 13693349888 | bytes 33767424 | tf_op jit(solution)/shard_map/dot_general | solution.py:42
  173.6 10.2 %fusion.1 = (f32[4096]{0:T(1024)S(1)}, f32[4096]{0:T(1024)S(1)}, f32[4096]{0:T(1024)S(1)}, f32[4096]{0:T(1024)S(1)}, f32[4096]{0:T(1024)S(1)}, /*index=5*/f32[4096]{0:T(1024)S(1)}) fusion(f32[4096,768]{0,1:T(8,128)S(1)} %bitcast.88, f32[4096]{0:T(1024)S(1)} %get-tuple-element.58, s32[4096]{0:T(1024)S(1)} %bitcast.98, s32[768]{0:T(1024)S(1)} %get-tuple-element.63, ...), kind=kLoop, calls=%fused_computation.7 | loop fusion | flops 44015616 | bytes 25319424 | tf_op jit(solution)/shard_map/reduce_sum | solution.py:45
  183.8 0.1 broadcast_select_fusion
  184.0 0.1 broadcast_select_fusion.1
  184.1 0.1 fusion.42
  184.2 0.1 fusion.20
  184.6 0.7 copy.45
  185.2 5.0 %all-to-all-start = ((f32[4,16,256]{2,0,1:T(4,128)}), f32[4,16,256]{2,0,1:T(4,128)S(1)}, u32[]{:S(2)}, u32[]{:S(2)}) async-start(f32[4,16,256]{2,0,1:T(4,128)} %bitcast.15), calls=%async_computation | async-start | bytes 131072 | tf_op jit(solution)/shard_map/all_to_all | solution.py:179
  190.9 7.0 %all-to-all-done = f32[4,16,256]{2,0,1:T(4,128)S(1)} async-done(((f32[4,16,256]{2,0,1:T(4,128)}), f32[4,16,256]{2,0,1:T(4,128)S(1)}, u32[]{:S(2)}, u32[]{:S(2)}) %all-to-all-start) | async-done | bytes 65568 | tf_op jit(solution)/shard_map/all_to_all | solution.py:179
  198.0 12.5 %all-gather.1 = f32[4,4,256]{2,1,0:T(4,128)S(1)} all-gather(f32[1,4,256]{2,1,0:T(4,128)S(1)} %maximum_bitcast_fusion), channel_id=2, replica_groups=mesh['x'=4,'z'=4,'core'=2,'tp'=4] {'tp'}, dimensions={0}, use_global_device_ids=true | all-gather | bytes 20480 | tf_op jit(solution)/shard_map/all_gather | solution.py:181
  210.5 1.3 fusion.41
  (28 shorter events, 0.5 us)
Async XLA Ops:
  123.7 20.6 %copy-start = (bf16[2048,768]{1,0:T(8,128)(2,1)S(1)}, bf16[2048,768]{1,0:T(8,128)(2,1)}, u32[]{:S(2)}) copy-start(bf16[2048,768]{1,0:T(8,128)(2,1)} %param.9) | copy-start | bytes 9437188
  152.9 20.7 %slice-start = ((s8[12582912]{0:T(1024)(128)(4,1)}), s8[4194304]{0:T(1024)(128)(4,1)S(1)}, s32[]{:S(2)}) async-start(s8[12582912]{0:T(1024)(128)(4,1)} %bitcast.87), calls=%async_computation.1 | async-start | bytes 8388608
  152.9 20.7 %slice-start.1 = ((s8[12582912]{0:T(1024)(128)(4,1)}), s8[4194304]{0:T(1024)(128)(4,1)S(1)}, s32[]{:S(2)}) async-start(s8[12582912]{0:T(1024)(128)(4,1)} %bitcast.87), calls=%async_computation.2 | async-start | bytes 8388608
  152.9 20.7 %slice-start.2 = ((s8[12582912]{0:T(1024)(128)(4,1)}), s8[4194304]{0:T(1024)(128)(4,1)S(1)}, s32[]{:S(2)}) async-start(s8[12582912]{0:T(1024)(128)(4,1)} %bitcast.87), calls=%async_computation.3 | async-start | bytes 8388608
  185.2 12.7 %all-to-all-start = ((f32[4,16,256]{2,0,1:T(4,128)}), f32[4,16,256]{2,0,1:T(4,128)S(1)}, u32[]{:S(2)}, u32[]{:S(2)}) async-start(f32[4,16,256]{2,0,1:T(4,128)} %bitcast.15), calls=%async_computation | async-start | bytes 131072 | tf_op jit(solution)/shard_map/all_to_all | solution.py:179
where the time goes:
time: 214 us
  Pallas kernels  122 us (57%)
  matrix products  41.3 us (19%)
  other arithmetic  18.5 us (9%)
  blocking collectives  12.5 us (6%)
  waiting for transfers between devices  7.02 us (3%)
  starting transfers between devices  4.98 us (2%)
  local copies, waits for them, and re-layouts  4.46 us (2%)
  between operations  3.35 us (2%)
    pallas_call x1, Pallas kernels, gather_plane(): pl.pallas_call(gather_kernel, out_shape=jax.ShapeDtypeStruct((4, 4, rows,...  115 us
    dot_general x2, matrix products, slice_stats(): logits = jnp.dot(block, matrix, preferred_element_type=jnp.float32)  41.3 us
    all_gather x1, blocking collectives, per_device(): everyone = lax.all_gather(own, 'tp', axis=0)  12.5 us
    reduce_sum x1, other arithmetic, slice_stats(): weight_sum = jnp.sum(shifted, axis=-1)  10.2 us
    all_to_all x1, waiting for transfers between devices, per_device(): lax.all_to_all(by_chip, ('x', 'z'), split_axis=1, concat_axis=1, tiled=True)  7.02 us
    pallas_call x1, Pallas kernels, swap_with_other_core(): pl.pallas_call(swap_kernel, out_shape=jax.ShapeDtypeStruct(head.shape, he...  6.3 us
    all_to_all x1, starting transfers between devices, per_device(): lax.all_to_all(by_chip, ('x', 'z'), split_axis=1, concat_axis=1, tiled=True)  4.98 us
  transfers between devices with their start and end apart: 1, of which 1 were waited for; matrix products, arithmetic and copies ran while one was open for 0% of the time, Pallas kernels for 0%

commit v1 on v0

--- a/solution.py
+++ b/solution.py
@@ -8,34 +8,6 @@
 
 MESH = pl.DeviceIdType.MESH
 EXTRA = 128
-
-
-def swap_kernel(src_ref, dst_ref, send_sem, recv_sem):
-    peer = (lax.axis_index("x"), lax.axis_index("z"), 1 - lax.axis_index("core"), lax.axis_index("tp"))
-    barrier = pltpu.get_barrier_semaphore()
-    pl.semaphore_signal(barrier, inc=1, device_id=peer, device_id_type=MESH)
-    pl.semaphore_wait(barrier, 1)
-    copy = pltpu.make_async_remote_copy(
-        src_ref=src_ref,
-        dst_ref=dst_ref,
-        send_sem=send_sem,
-        recv_sem=recv_sem,
-        device_id=peer,
-        device_id_type=MESH,
-    )
-    copy.start()
-    copy.wait()
-
-
-def swap_with_other_core(head):
-    return pl.pallas_call(
-        swap_kernel,
-        out_shape=jax.ShapeDtypeStruct(head.shape, head.dtype),
-        in_specs=[pl.BlockSpec(memory_space=pl.ANY)],
-        out_specs=pl.BlockSpec(memory_space=pl.ANY),
-        scratch_shapes=[pltpu.SemaphoreType.DMA, pltpu.SemaphoreType.DMA],
-        compiler_params=pltpu.CompilerParams(collective_id=0, has_side_effects=True),
-    )(head)
 
 
 def slice_stats(block, target, matrix, vocab_ids):
@@ -60,17 +32,28 @@
     )
 
 
-def gather_kernel(piece_ref, out_ref, own_sem, send_sems, recv_sems):
+def gather_kernel(piece_ref, head_ref, out_ref, other_ref, own_sem, head_sems, send_sems, recv_sems):
     xi, zi = lax.axis_index("x"), lax.axis_index("z")
     core, tp = lax.axis_index("core"), lax.axis_index("tp")
 
     def dev(dx, dz):
         return (lax.rem(xi + dx, 4), lax.rem(zi + dz, 4), core, tp)
 
+    partner = (xi, zi, 1 - core, tp)
     barrier = pltpu.get_barrier_semaphore()
     for dx, dz in ((1, 0), (3, 0), (0, 1), (0, 3)):
         pl.semaphore_signal(barrier, inc=1, device_id=dev(dx, dz), device_id_type=MESH)
-    pl.semaphore_wait(barrier, 4)
+    pl.semaphore_signal(barrier, inc=1, device_id=partner, device_id_type=MESH)
+    pl.semaphore_wait(barrier, 5)
+    swap = pltpu.make_async_remote_copy(
+        src_ref=head_ref,
+        dst_ref=other_ref,
+        send_sem=head_sems.at[0],
+        recv_sem=head_sems.at[1],
+        device_id=partner,
+        device_id_type=MESH,
+    )
+    swap.start()
     own = pltpu.make_async_copy(piece_ref, out_ref.at[0, 0], own_sem)
     own.start()
     rows = piece_ref.shape[0]
@@ -120,22 +103,115 @@
         send(out_ref.at[:, 3, h:h + q], out_ref.at[:, 2, h:h + q], 1, 0),
         send(out_ref.at[:, 1, h + q:rows], out_ref.at[:, 2, h + q:rows], 3, 0),
     ])
-
-
-def gather_plane(piece):
+    swap.wait()
+
+
+def gather_plane(piece, head):
     rows, cols = piece.shape
     return pl.pallas_call(
         gather_kernel,
-        out_shape=jax.ShapeDtypeStruct((4, 4, rows, cols), piece.dtype),
+        out_shape=(
+            jax.ShapeDtypeStruct((4, 4, rows, cols), piece.dtype),
+            jax.ShapeDtypeStruct(head.shape, head.dtype),
+        ),
+        in_specs=[pl.BlockSpec(memory_space=pl.ANY)] * 2,
+        out_specs=(pl.BlockSpec(memory_space=pl.ANY), pl.BlockSpec(memory_space=pl.ANY)),
+        scratch_shapes=[
+            pltpu.SemaphoreType.DMA,
+            pltpu.SemaphoreType.DMA((2,)),
+            pltpu.SemaphoreType.DMA((16,)),
+            pltpu.SemaphoreType.DMA((16,)),
+        ],
+        compiler_params=pltpu.CompilerParams(collective_id=1, has_side_effects=True),
+    )(piece, head)
+
+
+def plane_kernel(stats_ref, out_ref, own_sem, send_sems, recv_sems):
+    xi, zi = lax.axis_index("x"), lax.axis_index("z")
+    core, tp = lax.axis_index("core"), lax.axis_index("tp")
+    offsets = [(dx, dz) for dz in range(4) for dx in range(4) if dx or dz]
+    barrier = pltpu.get_barrier_semaphore()
+    for dx, dz in offsets:
+        peer = (lax.rem(xi + dx, 4), lax.rem(zi + dz, 4), core, tp)
+        pl.semaphore_signal(barrier, inc=1, device_id=peer, device_id_type=MESH)
+    pl.semaphore_wait(barrier, len(offsets))
+    own = pltpu.make_async_copy(stats_ref.at[0, 0], out_ref.at[0, 0], own_sem)
+    own.start()
+    cps = []
+    for k, (dx, dz) in enumerate(offsets):
+        peer = (lax.rem(xi + dx, 4), lax.rem(zi + dz, 4), core, tp)
+        cp = pltpu.make_async_remote_copy(
+            src_ref=stats_ref.at[dz, dx],
+            dst_ref=out_ref.at[(4 - dz) % 4, (4 - dx) % 4],
+            send_sem=send_sems.at[k],
+            recv_sem=recv_sems.at[k],
+            device_id=peer,
+            device_id_type=MESH,
+        )
+        cp.start()
+        cps.append(cp)
+    own.wait()
+    for cp in cps:
+        cp.wait()
+
+
+def exchange_plane(stats):
+    return pl.pallas_call(
+        plane_kernel,
+        out_shape=jax.ShapeDtypeStruct(stats.shape, stats.dtype),
         in_specs=[pl.BlockSpec(memory_space=pl.ANY)],
         out_specs=pl.BlockSpec(memory_space=pl.ANY),
         scratch_shapes=[
             pltpu.SemaphoreType.DMA,
-            pltpu.SemaphoreType.DMA((16,)),
-            pltpu.SemaphoreType.DMA((16,)),
+            pltpu.SemaphoreType.DMA((15,)),
+            pltpu.SemaphoreType.DMA((15,)),
         ],
-        compiler_params=pltpu.CompilerParams(collective_id=1, has_side_effects=True),
-    )(piece)
+        compiler_params=pltpu.CompilerParams(collective_id=2, has_side_effects=True),
+    )(stats)
+
+
+def tp_kernel(own_ref, out_ref, own_sem, send_sems, recv_sems):
+    xi, zi = lax.axis_index("x"), lax.axis_index("z")
+    core, tp = lax.axis_index("core"), lax.axis_index("tp")
+    n = out_ref.shape[0]
+    barrier = pltpu.get_barrier_semaphore()
+    for d in range(1, n):
+        peer = (xi, zi, core, lax.rem(tp + d, n))
+        pl.semaphore_signal(barrier, inc=1, device_id=peer, device_id_type=MESH)
+    pl.semaphore_wait(barrier, n - 1)
+    own = pltpu.make_async_copy(own_ref, out_ref.at[tp], own_sem)
+    own.start()
+    cps = []
+    for d in range(1, n):
+        peer = (xi, zi, core, lax.rem(tp + d, n))
+        cp = pltpu.make_async_remote_copy(
+            src_ref=own_ref,
+            dst_ref=out_ref.at[tp],
+            send_sem=send_sems.at[d - 1],
+            recv_sem=recv_sems.at[d - 1],
+            device_id=peer,
+            device_id_type=MESH,
+        )
+        cp.start()
+        cps.append(cp)
+    own.wait()
+    for cp in cps:
+        cp.wait()
+
+
+def exchange_tp(own, n_tp):
+    return pl.pallas_call(
+        tp_kernel,
+        out_shape=jax.ShapeDtypeStruct((n_tp, *own.shape), own.dtype),
+        in_specs=[pl.BlockSpec(memory_space=pl.ANY)],
+        out_specs=pl.BlockSpec(memory_space=pl.ANY),
+        scratch_shapes=[
+            pltpu.SemaphoreType.DMA,
+            pltpu.SemaphoreType.DMA((n_tp - 1,)),
+            pltpu.SemaphoreType.DMA((n_tp - 1,)),
+        ],
+        compiler_params=pltpu.CompilerParams(collective_id=3, has_side_effects=True),
+    )(own)
 
 
 def per_device(hidden_states, norm_gain, head, target_ids, lengths):
@@ -155,7 +231,6 @@
     tail = jnp.zeros((rows, EXTRA), jnp.bfloat16).at[:, :3].set(digits.astype(jnp.bfloat16))
     piece = jnp.concatenate([normed, tail], axis=1)
     head_ext = jnp.concatenate([head, jnp.zeros((EXTRA, vdev), head.dtype)], axis=0)
-    other_head = swap_with_other_core(head_ext)
     columns = lax.broadcasted_iota(jnp.int32, (1, vdev), 1)
     own_ids = columns + ((chip * 2 + core) * n_tp + tp) * vdev
     other_ids = columns + ((chip * 2 + 1 - core) * n_tp + tp) * vdev
@@ -172,13 +247,11 @@
         merged = jnp.stack(merge(jnp.stack([first, second]), axis=0))
         return merged.reshape(4, *lead, block.shape[-2])
 
-    gathered = gather_plane(piece)
+    gathered, other_head = gather_plane(piece, head_ext)
     rel = stats_of(gathered.reshape(-1, gathered.shape[-1])).reshape(4, 4, 4, rows)
-    absolute = jnp.roll(jnp.roll(rel, zi, axis=1), xi, axis=2)
-    by_chip = jnp.swapaxes(absolute, 1, 2).reshape(4, -1, rows)
-    arrived = lax.all_to_all(by_chip, ("x", "z"), split_axis=1, concat_axis=1, tiled=True)
-    own = jnp.stack(merge(jnp.moveaxis(arrived, 1, 0), axis=0))
-    everyone = lax.all_gather(own, "tp", axis=0)
+    arrived = exchange_plane(jnp.moveaxis(rel, 0, 2))
+    own = jnp.stack(merge(arrived.reshape(16, 4, rows), axis=0))
+    everyone = exchange_tp(own, n_tp)
     top, weight_sum, weighted, picked = merge(everyone, axis=0)
     log_norm = top + jnp.log(weight_sum)
     live = jnp.arange(rows, dtype=jnp.int32) < lengths[0]

time: 214 us -> 201 us (0.939)
  blocking collectives: 12.5 us -> 0 us
  Pallas kernels: 122 us -> 131 us
  waiting for transfers between devices: 7.02 us -> 0 us
  starting transfers between devices: 4.98 us -> 0 us
  other arithmetic: 18.5 us -> 21.7 us
    all_gather x1 -> x0, blocking collectives: 12.5 us -> none  [per_device(): everyone = lax.all_gather(own, 'tp', axis=0)]
    pallas_call x2 -> x3, Pallas kernels: 122 us -> 131 us  [the longest x1 116 us: gather_plane(): pl.pallas_call(gather_kernel, out_shape=(jax.ShapeDtypeStruct((4, 4, rows...]
    all_to_all x1 -> x0, waiting for transfers between devices: 7.02 us -> none  [per_device(): lax.all_to_all(by_chip, ('x', 'z'), split_axis=1, concat_axis=1, tiled=True)]
    all_to_all x1 -> x0, starting transfers between devices: 4.98 us -> none  [per_device(): lax.all_to_all(by_chip, ('x', 'z'), split_axis=1, concat_axis=1, tiled=True)]
  transfers between devices with their start and end apart: 1 -> 0, of which waited for: 1 -> 0; matrix products, arithmetic and copies ran while one was open for 0% -> 0% of each run, Pallas kernels for 0% -> 0%
where the time goes in v1:
time: 201 us; the launch traced here: 200 us
  Pallas kernels  131 us (65%)
  matrix products  41.1 us (20%)
  other arithmetic  21.7 us (11%)
  local copies, waits for them, and re-layouts  3.77 us (2%)
  between operations  3.32 us (2%)
    pallas_call x1, Pallas kernels, gather_plane(): pl.pallas_call(gather_kernel, out_shape=(jax.ShapeDtypeStruct((4, 4, rows...  116 us
    dot_general x2, matrix products, slice_stats(): logits = jnp.dot(block, matrix, preferred_element_type=jnp.float32)  41.1 us
    reduce_sum x1, other arithmetic, slice_stats(): weight_sum = jnp.sum(shifted, axis=-1)  10.2 us
    pallas_call x1, Pallas kernels, exchange_plane(): pl.pallas_call(plane_kernel, out_shape=jax.ShapeDtypeStruct(stats.shape,...  8.46 us
    pallas_call x1, Pallas kernels, exchange_tp(): pl.pallas_call(tp_kernel, out_shape=jax.ShapeDtypeStruct((n_tp, *own.shap...  6.52 us

profile of v1, /device:TPU:0, one launch (start us, length us, event | category | flops | bytes accessed | tf_op | source)
XLA Modules:
  0.0 200.5 jit_solution(13167560517980467962)
XLA Ops:
  0.7 0.8 fusion.27
  1.6 0.1 copy.33
  1.7 0.6 compare_reduce_fusion
  2.3 0.7 broadcast_select_fusion.2
  3.0 1.5 fusion.3
  4.5 1.5 fusion.5
  6.1 1.1 fusion.6.piece_ref
  7.1 1.9 concatenate.38.head_ref
  9.1 115.6 %shard_map.84 = (bf16[4,4,256,2176]{3,2,1,0:T(8,128)(2,1)}, bf16[2176,768]{1,0:T(8,128)(2,1)}) custom-call(bf16[256,2176]{1,0:T(8,128)(2,1)} %fusion.6.piece_ref, bf16[2176,768]{1,0:T(8,128)(2,1)} %concatenate.38.head_ref), custom_call_target="tpu_custom_call" | custom-call | tf_op jit(solution)/shard_map/pallas_call | solution.py:111
  124.7 20.5 %fusion.37 = (f32[4096]{0:T(1024)S(1)}, f32[4096,768]{0,1:T(8,128)}) fusion(bf16[4096,2176]{1,0:T(8,128)(2,1)} %bitcast.101, bf16[2176,768]{1,0:T(8,128)(2,1)} %get-tuple-element.19), kind=kOutput, calls=%fused_computation.98 | convolution fusion | flops 13693349888 | bytes 33767424 | tf_op jit(solution)/shard_map/dot_general | solution.py:14
  145.2 1.3 slice.83
  146.5 0.4 copy.41
  147.0 20.6 %fusion.38 = (f32[4096]{0:T(1024)S(1)}, f32[4096,768]{0,1:T(8,128)}) fusion(bf16[4096,2176]{1,0:T(8,128)(2,1)} %bitcast.103, bf16[2048,768]{1,0:T(8,128)(2,1)} %param.9), kind=kOutput, calls=%fused_computation.99 | convolution fusion | flops 13693349888 | bytes 33570816 | tf_op jit(solution)/shard_map/dot_general | solution.py:14
  167.6 10.2 %fusion = (f32[4096]{0:T(1024)S(1)}, f32[4096]{0:T(1024)S(1)}, f32[4096]{0:T(1024)S(1)}, f32[4096]{0:T(1024)S(1)}, f32[4096]{0:T(1024)S(1)}, /*index=5*/f32[4096]{0:T(1024)S(1)}) fusion(f32[4096,768]{0,1:T(8,128)S(1)} %bitcast.86, f32[4096]{0:T(1024)S(1)} %get-tuple-element.62, s32[4096]{0:T(1024)S(1)} %bitcast.97, s32[768]{0:T(1024)S(1)} %get-tuple-element.66, ...), kind=kLoop, calls=%fused_computation.3 | loop fusion | flops 44015616 | bytes 25319424 | tf_op jit(solution)/shard_map/reduce_sum | solution.py:17
  177.9 0.2 broadcast_select_fusion.1
  178.1 0.1 fusion.33
  178.3 0.1 fusion.13
  178.4 0.7 maximum_bitcast_fusion.stats_ref
  179.1 8.5 %shard_map.85 = f32[4,4,4,256]{3,2,1,0:T(4,128)} custom-call(f32[4,4,4,256]{3,2,1,0:T(4,128)} %maximum_bitcast_fusion.stats_ref), custom_call_target="tpu_custom_call" | custom-call | tf_op jit(solution)/shard_map/pallas_call | solution.py:159
  187.6 1.1 fusion.35
  188.7 0.6 pad_maximum_fusion.3.own_ref
  189.3 6.5 %shard_map.86 = f32[4,4,256]{2,1,0:T(4,128)} custom-call(f32[4,256]{1,0:T(4,128)} %pad_maximum_fusion.3.own_ref), custom_call_target="tpu_custom_call" | custom-call | tf_op jit(solution)/shard_map/pallas_call | solution.py:203
  195.8 0.9 fusion.36
  197.4 1.3 fusion.32
  (20 shorter events, 0.2 us)
Async XLA Ops:
  0.6 6.5 %copy-start = (bf16[2048,768]{1,0:T(8,128)(2,1)S(1)}, bf16[2048,768]{1,0:T(8,128)(2,1)}, u32[]{:S(2)}) copy-start(bf16[2048,768]{1,0:T(8,128)(2,1)} %param.9) | copy-start | bytes 9437188
  147.0 20.6 %slice-start = ((s8[12582912]{0:T(1024)(128)(4,1)}), s8[4194304]{0:T(1024)(128)(4,1)S(1)}, s32[]{:S(2)}) async-start(s8[12582912]{0:T(1024)(128)(4,1)} %bitcast.85), calls=%async_computation | async-start | bytes 8388608
  147.0 20.6 %slice-start.1 = ((s8[12582912]{0:T(1024)(128)(4,1)}), s8[4194304]{0:T(1024)(128)(4,1)S(1)}, s32[]{:S(2)}) async-start(s8[12582912]{0:T(1024)(128)(4,1)} %bitcast.85), calls=%async_computation.1 | async-start | bytes 8388608
  147.0 20.6 %slice-start.2 = ((s8[12582912]{0:T(1024)(128)(4,1)}), s8[4194304]{0:T(1024)(128)(4,1)S(1)}, s32[]{:S(2)}) async-start(s8[12582912]{0:T(1024)(128)(4,1)} %bitcast.85), calls=%async_computation.2 | async-start | bytes 8388608

commit v2 on v1

--- a/solution.py
+++ b/solution.py
@@ -1,3 +1,5 @@
+import functools
+
 import jax
 import jax.numpy as jnp
 import numpy as np
@@ -32,9 +34,11 @@
     )
 
 
-def gather_kernel(piece_ref, head_ref, out_ref, other_ref, own_sem, head_sems, send_sems, recv_sems):
+def fused_kernel(n_tp, piece_ref, head_ref, sel_ref, out_ref, stats_ref,
+                 hboth, vbuf, local_sems, head_sems, send_sems, recv_sems, load_sems):
     xi, zi = lax.axis_index("x"), lax.axis_index("z")
     core, tp = lax.axis_index("core"), lax.axis_index("tp")
+    vdev = head_ref.shape[0]
 
     def dev(dx, dz):
         return (lax.rem(xi + dx, 4), lax.rem(zi + dz, 4), core, tp)
@@ -45,16 +49,21 @@
         pl.semaphore_signal(barrier, inc=1, device_id=dev(dx, dz), device_id_type=MESH)
     pl.semaphore_signal(barrier, inc=1, device_id=partner, device_id_type=MESH)
     pl.semaphore_wait(barrier, 5)
+    mine = pl.ds(pl.multiple_of(core * vdev, vdev), vdev)
     swap = pltpu.make_async_remote_copy(
         src_ref=head_ref,
-        dst_ref=other_ref,
+        dst_ref=hboth.at[mine],
         send_sem=head_sems.at[0],
         recv_sem=head_sems.at[1],
         device_id=partner,
         device_id_type=MESH,
     )
     swap.start()
-    own = pltpu.make_async_copy(piece_ref, out_ref.at[0, 0], own_sem)
+    own_head = pltpu.make_async_copy(head_ref, hboth.at[mine], local_sems.at[0])
+    own_head.start()
+    sel = pltpu.make_async_copy(sel_ref, hboth.at[pl.ds(2 * vdev, sel_ref.shape[0])], local_sems.at[1])
+    sel.start()
+    own = pltpu.make_async_copy(piece_ref, out_ref.at[0, 0], local_sems.at[2])
     own.start()
     rows = piece_ref.shape[0]
     h, q = rows // 2, rows // 4
@@ -78,6 +87,46 @@
         for cp in cps:
             cp.wait()
 
+    chip = xi * 4 + zi
+    ids = lax.broadcasted_iota(jnp.int32, (2 * vdev, 1), 0)
+    vocab = (((chip * 2 + ids // vdev) * n_tp + tp) * vdev + ids % vdev).astype(jnp.float32)
+
+    def group(m, half):
+        off = lax.rem(m * 3, 4)
+        loads = []
+        for j in range(4):
+            if half == 0:
+                src = out_ref.at[off, j, pl.ds(0, h)]
+            else:
+                src = out_ref.at[j, off, pl.ds(h, h)]
+            cp = pltpu.make_async_copy(src, vbuf.at[j], load_sems.at[j])
+            cp.start()
+            loads.append(cp)
+        finish(loads)
+        block = vbuf[...].reshape(4 * h, vbuf.shape[2])
+        logits = lax.dot_general(
+            hboth[...], block, (((1,), (1,)), ((), ())), preferred_element_type=jnp.float32
+        )
+        real = logits[: 2 * vdev]
+        code = logits[2 * vdev: 2 * vdev + 8]
+        target = code[0:1] + code[1:2] * 64.0 + code[2:3] * 4096.0
+        top = jnp.max(real, axis=0, keepdims=True)
+        shifted = jnp.exp(real - top)
+        g = m * 2 + half
+        stats_ref[g, 0:1, :] = top
+        stats_ref[g, 1:2, :] = jnp.sum(shifted, axis=0, keepdims=True)
+        stats_ref[g, 2:3, :] = jnp.sum(shifted * real, axis=0, keepdims=True)
+        stats_ref[g, 3:4, :] = jnp.sum(jnp.where(vocab == target, real, 0.0), axis=0, keepdims=True)
+
+    def phase(ms):
+        def body(i, carry):
+            m = ms[0] + i * (ms[1] - ms[0]) if len(ms) > 1 else ms[0] + i * 0
+            group(m, 0)
+            group(m, 1)
+            return carry
+
+        lax.fori_loop(0, len(ms), body, 0)
+
     finish([
         send(piece_ref.at[0:h], out_ref.at[0, 3, 0:h], 1, 0),
         send(piece_ref.at[0:h], out_ref.at[0, 1, 0:h], 3, 0),
@@ -91,39 +140,53 @@
         send(out_ref.at[1, 0, h + q:rows], out_ref.at[2, 0, h + q:rows], 0, 3),
     ])
     own.wait()
-    finish([
+    third = [
         send(out_ref.at[0, :, 0:h], out_ref.at[3, :, 0:h], 0, 1),
         send(out_ref.at[0, :, 0:h], out_ref.at[1, :, 0:h], 0, 3),
         send(out_ref.at[:, 0, h:rows], out_ref.at[:, 3, h:rows], 1, 0),
         send(out_ref.at[:, 0, h:rows], out_ref.at[:, 1, h:rows], 3, 0),
-    ])
-    finish([
+    ]
+    swap.wait()
+    own_head.wait()
+    sel.wait()
+    phase((0,))
+    finish(third)
+    fourth = [
         send(out_ref.at[3, :, 0:q], out_ref.at[2, :, 0:q], 0, 1),
         send(out_ref.at[1, :, q:h], out_ref.at[2, :, q:h], 0, 3),
         send(out_ref.at[:, 3, h:h + q], out_ref.at[:, 2, h:h + q], 1, 0),
         send(out_ref.at[:, 1, h + q:rows], out_ref.at[:, 2, h + q:rows], 3, 0),
-    ])
-    swap.wait()
-
-
-def gather_plane(piece, head):
+    ]
+    phase((1, 3))
+    finish(fourth)
+    phase((2,))
+
+
+def gather_and_stats(piece, head_t, sel, n_tp):
     rows, cols = piece.shape
+    vdev = head_t.shape[0]
+    h = rows // 2
     return pl.pallas_call(
-        gather_kernel,
+        functools.partial(fused_kernel, n_tp),
         out_shape=(
             jax.ShapeDtypeStruct((4, 4, rows, cols), piece.dtype),
-            jax.ShapeDtypeStruct(head.shape, head.dtype),
+            jax.ShapeDtypeStruct((8, 8, 4 * h), jnp.float32),
         ),
-        in_specs=[pl.BlockSpec(memory_space=pl.ANY)] * 2,
-        out_specs=(pl.BlockSpec(memory_space=pl.ANY), pl.BlockSpec(memory_space=pl.ANY)),
+        in_specs=[pl.BlockSpec(memory_space=pl.ANY)] * 3,
+        out_specs=(pl.BlockSpec(memory_space=pl.ANY), pl.BlockSpec(memory_space=pltpu.VMEM)),
         scratch_shapes=[
-            pltpu.SemaphoreType.DMA,
+            pltpu.VMEM((2 * vdev + sel.shape[0], cols), jnp.bfloat16),
+            pltpu.VMEM((4, h, cols), jnp.bfloat16),
+            pltpu.SemaphoreType.DMA((3,)),
             pltpu.SemaphoreType.DMA((2,)),
             pltpu.SemaphoreType.DMA((16,)),
             pltpu.SemaphoreType.DMA((16,)),
+            pltpu.SemaphoreType.DMA((4,)),
         ],
-        compiler_params=pltpu.CompilerParams(collective_id=1, has_side_effects=True),
-    )(piece, head)
+        compiler_params=pltpu.CompilerParams(
+            collective_id=1, has_side_effects=True, vmem_limit_bytes=60 * 1024 * 1024
+        ),
+    )(piece, head_t, sel)
 
 
 def plane_kernel(stats_ref, out_ref, own_sem, send_sems, recv_sems):
@@ -230,25 +293,15 @@
     digits = jnp.stack([target_ids % 64, (target_ids // 64) % 64, target_ids // 4096], axis=1)
     tail = jnp.zeros((rows, EXTRA), jnp.bfloat16).at[:, :3].set(digits.astype(jnp.bfloat16))
     piece = jnp.concatenate([normed, tail], axis=1)
-    head_ext = jnp.concatenate([head, jnp.zeros((EXTRA, vdev), head.dtype)], axis=0)
-    columns = lax.broadcasted_iota(jnp.int32, (1, vdev), 1)
-    own_ids = columns + ((chip * 2 + core) * n_tp + tp) * vdev
-    other_ids = columns + ((chip * 2 + 1 - core) * n_tp + tp) * vdev
-
-    def stats_of(block):
-        lead = block.shape[:-2]
-        flat = block.reshape(-1, block.shape[-1])
-        code = flat[:, dim:dim + 3].astype(jnp.int32)
-        target = code[:, 0] + code[:, 1] * 64 + code[:, 2] * 4096
-        s_own = slice_stats(flat, target, head_ext, own_ids)
-        s_other = slice_stats(flat, target, other_head, other_ids)
-        first = jnp.where(core == 0, s_own, s_other)
-        second = jnp.where(core == 0, s_other, s_own)
-        merged = jnp.stack(merge(jnp.stack([first, second]), axis=0))
-        return merged.reshape(4, *lead, block.shape[-2])
-
-    gathered, other_head = gather_plane(piece, head_ext)
-    rel = stats_of(gathered.reshape(-1, gathered.shape[-1])).reshape(4, 4, 4, rows)
+    head_t = jnp.concatenate([head, jnp.zeros((EXTRA, vdev), head.dtype)], axis=0).T
+    sel = jnp.zeros((8, dim + EXTRA), jnp.bfloat16).at[jnp.arange(3), dim + jnp.arange(3)].set(1.0)
+    _, stats = gather_and_stats(piece, head_t, sel, n_tp)
+    h = rows // 2
+    order = jnp.array([0, 3, 2, 1])
+    st = stats[:, :4].reshape(4, 2, 4, 4, h)
+    s_a = jnp.transpose(st[:, 0], (1, 0, 2, 3))[:, order]
+    s_b = jnp.transpose(st[:, 1], (1, 2, 0, 3))[:, :, order]
+    rel = jnp.concatenate([s_a, s_b], axis=3)
     arrived = exchange_plane(jnp.moveaxis(rel, 0, 2))
     own = jnp.stack(merge(arrived.reshape(16, 4, rows), axis=0))
     everyone = exchange_tp(own, n_tp)

time: 201 us -> 166 us (0.83)
  matrix products: 41.1 us -> 0 us
  Pallas kernels: 131 us -> 143 us
  other arithmetic: 21.7 us -> 10.7 us
  local copies, waits for them, and re-layouts: 3.77 us -> 8.77 us
    dot_general x2 -> x0, matrix products: 41.1 us -> none  [slice_stats(): logits = jnp.dot(block, matrix, preferred_element_type=jnp.float32)]
    pallas_call x1, Pallas kernels: 116 us -> 128 us  [gather_and_stats(): pl.pallas_call(functools.partial(fused_kernel, n_tp), out_shape=(jax.Shap...]
    reduce_sum x1 -> x0, other arithmetic: 10.2 us -> none  [slice_stats(): weight_sum = jnp.sum(shifted, axis=-1)]
    unnamed x9 -> x5, local copies, waits for them, and re-layouts: 0.4 us -> 3.79 us
where the time goes in v2:
time: 166 us
  Pallas kernels  143 us (86%)
  other arithmetic  10.7 us (6%)
  local copies, waits for them, and re-layouts  8.77 us (5%)
  between operations  3.28 us (2%)
    pallas_call x1, Pallas kernels, gather_and_stats(): pl.pallas_call(functools.partial(fused_kernel, n_tp), out_shape=(jax.Shap...  128 us
    pallas_call x1, Pallas kernels, exchange_plane(): pl.pallas_call(plane_kernel, out_shape=jax.ShapeDtypeStruct(stats.shape,...  8.46 us
    pallas_call x1, Pallas kernels, exchange_tp(): pl.pallas_call(tp_kernel, out_shape=jax.ShapeDtypeStruct((n_tp, *own.shap...  6.52 us
    unnamed x5, local copies, waits for them, and re-layouts  3.79 us

profile of v2, /device:TPU:0, one launch (start us, length us, event | category | flops | bytes accessed | tf_op | source)
XLA Modules:
  0.0 165.7 jit_solution(3159628563521066674)
XLA Ops:
  0.6 0.7 fusion.16
  1.4 0.1 copy.27
  1.5 0.6 compare_reduce_fusion
  2.2 0.7 broadcast_select_fusion
  2.8 1.5 fusion.1
  4.3 1.5 fusion.3
  5.9 1.1 fusion.4.piece_ref
  7.0 3.2 %copy.28 = bf16[2048,768]{0,1:T(8,128)(2,1)S(1)} copy(bf16[2048,768]{1,0:T(8,128)(2,1)} %param.10) | data formatting | bytes 6291456 | tf_op args[2]
  10.2 2.0 %pad_bitcast_fusion.head_ref = bf16[768,2176]{1,0:T(8,128)(2,1)} fusion(bf16[2048,768]{0,1:T(8,128)(2,1)S(1)} %copy.28), kind=kLoop, calls=%fused_computation.3 | loop fusion | bytes 6488064 | tf_op jit(solution)/shard_map/transpose | solution.py:296
  12.2 0.7 scatter_fusion
  12.9 0.0 copy-start
  12.9 0.6 copy-done
  13.5 128.0 %shard_map.93 = (bf16[4,4,256,2176]{3,2,1,0:T(8,128)(2,1)}, f32[8,8,512]{2,1,0:T(8,128)}) custom-call(bf16[256,2176]{1,0:T(8,128)(2,1)} %fusion.4.piece_ref, bf16[768,2176]{1,0:T(8,128)(2,1)} %pad_bitcast_fusion.head_ref, bf16[8,2176]{1,0:T(8,128)(2,1)} %copy-done), custom_call_target="tpu_custom_call" | custom-call | tf_op jit(solution)/shard_map/pallas_call | solution.py:169
  141.5 0.9 slice.51
  142.5 0.0 copy-done.1
  142.5 0.6 gather_fusion.1
  143.1 0.6 gather_fusion
  143.7 0.6 maximum_bitcast_fusion.stats_ref
  144.3 8.5 %shard_map.94 = f32[4,4,4,256]{3,2,1,0:T(4,128)} custom-call(f32[4,4,4,256]{3,2,1,0:T(4,128)} %maximum_bitcast_fusion.stats_ref), custom_call_target="tpu_custom_call" | custom-call | tf_op jit(solution)/shard_map/pallas_call | solution.py:222
  152.8 1.1 fusion.23
  153.9 0.6 pad_maximum_fusion.own_ref
  154.5 6.5 %shard_map.95 = f32[4,4,256]{2,1,0:T(4,128)} custom-call(f32[4,256]{1,0:T(4,128)} %pad_maximum_fusion.own_ref), custom_call_target="tpu_custom_call" | custom-call | tf_op jit(solution)/shard_map/pallas_call | solution.py:266
  161.0 0.9 fusion.25
  162.6 1.3 fusion.22
  (17 shorter events, 0.2 us)
Async XLA Ops:
  12.9 0.6 copy-start
  13.5 129.0 %copy-start.1 = (s32[4]{0:T(128)S(1)}, s32[4]{0:T(128)}, u32[]{:S(2)}) copy-start(s32[4]{0:T(128)} %constant.128) | copy-start | bytes 52

commit v3 on v2

--- a/solution.py
+++ b/solution.py
@@ -91,19 +91,17 @@
     ids = lax.broadcasted_iota(jnp.int32, (2 * vdev, 1), 0)
     vocab = (((chip * 2 + ids // vdev) * n_tp + tp) * vdev + ids % vdev).astype(jnp.float32)
 
-    def group(m, half):
-        off = lax.rem(m * 3, 4)
+    def group(off, half, sub):
         loads = []
+        r0 = half * h + sub * q
         for j in range(4):
-            if half == 0:
-                src = out_ref.at[off, j, pl.ds(0, h)]
-            else:
-                src = out_ref.at[j, off, pl.ds(h, h)]
-            cp = pltpu.make_async_copy(src, vbuf.at[j], load_sems.at[j])
+            dz = off * (1 - half) + j * half
+            dx = j * (1 - half) + off * half
+            cp = pltpu.make_async_copy(out_ref.at[dz, dx, pl.ds(r0, q)], vbuf.at[j], load_sems.at[j])
             cp.start()
             loads.append(cp)
         finish(loads)
-        block = vbuf[...].reshape(4 * h, vbuf.shape[2])
+        block = vbuf[...].reshape(4 * q, vbuf.shape[2])
         logits = lax.dot_general(
             hboth[...], block, (((1,), (1,)), ((), ())), preferred_element_type=jnp.float32
         )
@@ -112,20 +110,18 @@
         target = code[0:1] + code[1:2] * 64.0 + code[2:3] * 4096.0
         top = jnp.max(real, axis=0, keepdims=True)
         shifted = jnp.exp(real - top)
-        g = m * 2 + half
+        g = (off * 2 + half) * 2 + sub
         stats_ref[g, 0:1, :] = top
         stats_ref[g, 1:2, :] = jnp.sum(shifted, axis=0, keepdims=True)
         stats_ref[g, 2:3, :] = jnp.sum(shifted * real, axis=0, keepdims=True)
         stats_ref[g, 3:4, :] = jnp.sum(jnp.where(vocab == target, real, 0.0), axis=0, keepdims=True)
 
-    def phase(ms):
+    def run(count, pick):
         def body(i, carry):
-            m = ms[0] + i * (ms[1] - ms[0]) if len(ms) > 1 else ms[0] + i * 0
-            group(m, 0)
-            group(m, 1)
+            group(*pick(i))
             return carry
 
-        lax.fori_loop(0, len(ms), body, 0)
+        lax.fori_loop(0, count, body, 0)
 
     finish([
         send(piece_ref.at[0:h], out_ref.at[0, 3, 0:h], 1, 0),
@@ -140,26 +136,34 @@
         send(out_ref.at[1, 0, h + q:rows], out_ref.at[2, 0, h + q:rows], 0, 3),
     ])
     own.wait()
-    third = [
-        send(out_ref.at[0, :, 0:h], out_ref.at[3, :, 0:h], 0, 1),
-        send(out_ref.at[0, :, 0:h], out_ref.at[1, :, 0:h], 0, 3),
-        send(out_ref.at[:, 0, h:rows], out_ref.at[:, 3, h:rows], 1, 0),
-        send(out_ref.at[:, 0, h:rows], out_ref.at[:, 1, h:rows], 3, 0),
-    ]
+    third = []
+    for lo, hi in ((0, q), (q, h)):
+        third.append([
+            send(out_ref.at[0, :, lo:hi], out_ref.at[3, :, lo:hi], 0, 1),
+            send(out_ref.at[0, :, lo:hi], out_ref.at[1, :, lo:hi], 0, 3),
+            send(out_ref.at[:, 0, h + lo:h + hi], out_ref.at[:, 3, h + lo:h + hi], 1, 0),
+            send(out_ref.at[:, 0, h + lo:h + hi], out_ref.at[:, 1, h + lo:h + hi], 3, 0),
+        ])
     swap.wait()
     own_head.wait()
     sel.wait()
-    phase((0,))
-    finish(third)
-    fourth = [
+    run(4, lambda i: (0, i // 2, i % 2))
+    finish(third[0])
+    fourth_a = [
         send(out_ref.at[3, :, 0:q], out_ref.at[2, :, 0:q], 0, 1),
+        send(out_ref.at[:, 3, h:h + q], out_ref.at[:, 2, h:h + q], 1, 0),
+    ]
+    run(4, lambda i: (3 - 2 * (i % 2), i // 2, 0))
+    finish(third[1])
+    fourth_b = [
         send(out_ref.at[1, :, q:h], out_ref.at[2, :, q:h], 0, 3),
-        send(out_ref.at[:, 3, h:h + q], out_ref.at[:, 2, h:h + q], 1, 0),
         send(out_ref.at[:, 1, h + q:rows], out_ref.at[:, 2, h + q:rows], 3, 0),
     ]
-    phase((1, 3))
-    finish(fourth)
-    phase((2,))
+    run(4, lambda i: (3 - 2 * (i % 2), i // 2, 1))
+    finish(fourth_a)
+    run(2, lambda i: (2, i, 0))
+    finish(fourth_b)
+    run(2, lambda i: (2, i, 1))
 
 
 def gather_and_stats(piece, head_t, sel, n_tp):
@@ -170,17 +174,17 @@
         functools.partial(fused_kernel, n_tp),
         out_shape=(
             jax.ShapeDtypeStruct((4, 4, rows, cols), piece.dtype),
-            jax.ShapeDtypeStruct((8, 8, 4 * h), jnp.float32),
+            jax.ShapeDtypeStruct((16, 8, 2 * h), jnp.float32),
         ),
         in_specs=[pl.BlockSpec(memory_space=pl.ANY)] * 3,
         out_specs=(pl.BlockSpec(memory_space=pl.ANY), pl.BlockSpec(memory_space=pltpu.VMEM)),
         scratch_shapes=[
             pltpu.VMEM((2 * vdev + sel.shape[0], cols), jnp.bfloat16),
-            pltpu.VMEM((4, h, cols), jnp.bfloat16),
+            pltpu.VMEM((4, h // 2, cols), jnp.bfloat16),
             pltpu.SemaphoreType.DMA((3,)),
             pltpu.SemaphoreType.DMA((2,)),
-            pltpu.SemaphoreType.DMA((16,)),
-            pltpu.SemaphoreType.DMA((16,)),
+            pltpu.SemaphoreType.DMA((20,)),
+            pltpu.SemaphoreType.DMA((20,)),
             pltpu.SemaphoreType.DMA((4,)),
         ],
         compiler_params=pltpu.CompilerParams(
@@ -296,11 +300,10 @@
     head_t = jnp.concatenate([head, jnp.zeros((EXTRA, vdev), head.dtype)], axis=0).T
     sel = jnp.zeros((8, dim + EXTRA), jnp.bfloat16).at[jnp.arange(3), dim + jnp.arange(3)].set(1.0)
     _, stats = gather_and_stats(piece, head_t, sel, n_tp)
-    h = rows // 2
-    order = jnp.array([0, 3, 2, 1])
-    st = stats[:, :4].reshape(4, 2, 4, 4, h)
-    s_a = jnp.transpose(st[:, 0], (1, 0, 2, 3))[:, order]
-    s_b = jnp.transpose(st[:, 1], (1, 2, 0, 3))[:, :, order]
+    q = rows // 4
+    st = stats[:, :4].reshape(4, 2, 2, 4, 4, q)
+    s_a = jnp.transpose(st[:, 0], (2, 0, 3, 1, 4)).reshape(4, 4, 4, 2 * q)
+    s_b = jnp.transpose(st[:, 1], (2, 3, 0, 1, 4)).reshape(4, 4, 4, 2 * q)
     rel = jnp.concatenate([s_a, s_b], axis=3)
     arrived = exchange_plane(jnp.moveaxis(rel, 0, 2))
     own = jnp.stack(merge(arrived.reshape(16, 4, rows), axis=0))

time: 166 us -> 168 us (1.012)
  Pallas kernels: 143 us -> 146 us
    pallas_call x1, Pallas kernels: 128 us -> 131 us  [gather_and_stats(): pl.pallas_call(functools.partial(fused_kernel, n_tp), out_shape=(jax.Shap...]
where the time goes in v3:
time: 168 us
  Pallas kernels  146 us (87%)
  other arithmetic  10.7 us (6%)
  local copies, waits for them, and re-layouts  7.95 us (5%)
  between operations  3.25 us (2%)
    pallas_call x1, Pallas kernels, gather_and_stats(): pl.pallas_call(functools.partial(fused_kernel, n_tp), out_shape=(jax.Shap...  131 us
    pallas_call x1, Pallas kernels, exchange_plane(): pl.pallas_call(plane_kernel, out_shape=jax.ShapeDtypeStruct(stats.shape,...  8.35 us
    pallas_call x1, Pallas kernels, exchange_tp(): pl.pallas_call(tp_kernel, out_shape=jax.ShapeDtypeStruct((n_tp, *own.shap...  6.51 us
    unnamed x5, local copies, waits for them, and re-layouts  3.86 us

profile of v3, /device:TPU:0, one launch (start us, length us, event | category | flops | bytes accessed | tf_op | source)
XLA Modules:
  0.0 167.5 jit_solution(18394798417940248617)
XLA Ops:
  0.6 0.7 fusion.16
  1.4 0.1 copy.26
  1.5 0.6 compare_reduce_fusion
  2.2 0.7 broadcast_select_fusion
  2.8 1.5 fusion.1
  4.3 1.5 fusion.3
  5.9 1.1 fusion.4.piece_ref
  7.0 3.2 %copy.27 = bf16[2048,768]{0,1:T(8,128)(2,1)S(1)} copy(bf16[2048,768]{1,0:T(8,128)(2,1)} %param.9) | data formatting | bytes 6291456 | tf_op args[2]
  10.2 2.0 %pad_bitcast_fusion.head_ref = bf16[768,2176]{1,0:T(8,128)(2,1)} fusion(bf16[2048,768]{0,1:T(8,128)(2,1)S(1)} %copy.27), kind=kLoop, calls=%fused_computation.1 | loop fusion | bytes 6488064 | tf_op jit(solution)/shard_map/transpose | solution.py:300
  12.2 0.7 scatter_fusion
  12.9 0.0 copy-start
  12.9 0.6 copy-done
  13.5 130.8 %shard_map.84 = (bf16[4,4,256,2176]{3,2,1,0:T(8,128)(2,1)}, f32[16,8,256]{2,1,0:T(8,128)}) custom-call(bf16[256,2176]{1,0:T(8,128)(2,1)} %fusion.4.piece_ref, bf16[768,2176]{1,0:T(8,128)(2,1)} %pad_bitcast_fusion.head_ref, bf16[8,2176]{1,0:T(8,128)(2,1)} %copy-done), custom_call_target="tpu_custom_call" | custom-call | tf_op jit(solution)/shard_map/pallas_call | solution.py:173
  144.3 0.9 slice.51
  145.2 0.1 reshape.82
  145.4 0.1 reshape.83
  145.5 0.1 reshape.84
  145.6 0.6 maximum_bitcast_fusion.stats_ref
  146.3 8.3 %shard_map.85 = f32[4,4,4,256]{3,2,1,0:T(4,128)} custom-call(f32[4,4,4,256]{3,2,1,0:T(4,128)} %maximum_bitcast_fusion.stats_ref), custom_call_target="tpu_custom_call" | custom-call | tf_op jit(solution)/shard_map/pallas_call | solution.py:226
  154.6 1.1 fusion.24
  155.7 0.6 pad_maximum_fusion.own_ref
  156.3 6.5 %shard_map.86 = f32[4,4,256]{2,1,0:T(4,128)} custom-call(f32[4,256]{1,0:T(4,128)} %pad_maximum_fusion.own_ref), custom_call_target="tpu_custom_call" | custom-call | tf_op jit(solution)/shard_map/pallas_call | solution.py:270
  162.8 0.9 fusion.25
  164.4 1.3 fusion.22
  (13 shorter events, 0.2 us)
Async XLA Ops:
  12.9 0.6 copy-start

commit v4 on v2

--- a/solution.py
+++ b/solution.py
@@ -34,8 +34,8 @@
     )
 
 
-def fused_kernel(n_tp, piece_ref, head_ref, sel_ref, out_ref, stats_ref,
-                 hboth, vbuf, local_sems, head_sems, send_sems, recv_sems, load_sems):
+def fused_kernel(n_tp, piece_ref, head_ref, tin_ref, out_ref, stats_ref,
+                 hboth, vbuf, tgt, local_sems, head_sems, send_sems, recv_sems, load_sems):
     xi, zi = lax.axis_index("x"), lax.axis_index("z")
     core, tp = lax.axis_index("core"), lax.axis_index("tp")
     vdev = head_ref.shape[0]
@@ -61,7 +61,7 @@
     swap.start()
     own_head = pltpu.make_async_copy(head_ref, hboth.at[mine], local_sems.at[0])
     own_head.start()
-    sel = pltpu.make_async_copy(sel_ref, hboth.at[pl.ds(2 * vdev, sel_ref.shape[0])], local_sems.at[1])
+    sel = pltpu.make_async_copy(tin_ref, tgt.at[0, 0], local_sems.at[1])
     sel.start()
     own = pltpu.make_async_copy(piece_ref, out_ref.at[0, 0], local_sems.at[2])
     own.start()
@@ -104,12 +104,14 @@
             loads.append(cp)
         finish(loads)
         block = vbuf[...].reshape(4 * h, vbuf.shape[2])
-        logits = lax.dot_general(
+        real = lax.dot_general(
             hboth[...], block, (((1,), (1,)), ((), ())), preferred_element_type=jnp.float32
         )
-        real = logits[: 2 * vdev]
-        code = logits[2 * vdev: 2 * vdev + 8]
-        target = code[0:1] + code[1:2] * 64.0 + code[2:3] * 4096.0
+        if half == 0:
+            pieces = [tgt[off, j, 0, 0:1, :] for j in range(4)]
+        else:
+            pieces = [tgt[j, off, 1, 0:1, :] for j in range(4)]
+        target = jnp.concatenate(pieces, axis=1)
         top = jnp.max(real, axis=0, keepdims=True)
         shifted = jnp.exp(real - top)
         g = m * 2 + half
@@ -132,23 +134,33 @@
         send(piece_ref.at[0:h], out_ref.at[0, 1, 0:h], 3, 0),
         send(piece_ref.at[h:rows], out_ref.at[3, 0, h:rows], 0, 1),
         send(piece_ref.at[h:rows], out_ref.at[1, 0, h:rows], 0, 3),
+        send(tin_ref.at[0], tgt.at[0, 3, 0], 1, 0),
+        send(tin_ref.at[0], tgt.at[0, 1, 0], 3, 0),
+        send(tin_ref.at[1], tgt.at[3, 0, 1], 0, 1),
+        send(tin_ref.at[1], tgt.at[1, 0, 1], 0, 3),
     ])
     finish([
         send(out_ref.at[0, 3, 0:q], out_ref.at[0, 2, 0:q], 1, 0),
         send(out_ref.at[0, 1, q:h], out_ref.at[0, 2, q:h], 3, 0),
         send(out_ref.at[3, 0, h:h + q], out_ref.at[2, 0, h:h + q], 0, 1),
         send(out_ref.at[1, 0, h + q:rows], out_ref.at[2, 0, h + q:rows], 0, 3),
+        send(tgt.at[0, 3, 0], tgt.at[0, 2, 0], 1, 0),
+        send(tgt.at[3, 0, 1], tgt.at[2, 0, 1], 0, 1),
     ])
     own.wait()
+    sel.wait()
     third = [
         send(out_ref.at[0, :, 0:h], out_ref.at[3, :, 0:h], 0, 1),
         send(out_ref.at[0, :, 0:h], out_ref.at[1, :, 0:h], 0, 3),
         send(out_ref.at[:, 0, h:rows], out_ref.at[:, 3, h:rows], 1, 0),
         send(out_ref.at[:, 0, h:rows], out_ref.at[:, 1, h:rows], 3, 0),
+        send(tgt.at[0, :, 0], tgt.at[3, :, 0], 0, 1),
+        send(tgt.at[0, :, 0], tgt.at[1, :, 0], 0, 3),
+        send(tgt.at[:, 0, 1], tgt.at[:, 3, 1], 1, 0),
+        send(tgt.at[:, 0, 1], tgt.at[:, 1, 1], 3, 0),
     ]
     swap.wait()
     own_head.wait()
-    sel.wait()
     phase((0,))
     finish(third)
     fourth = [
@@ -156,13 +168,15 @@
         send(out_ref.at[1, :, q:h], out_ref.at[2, :, q:h], 0, 3),
         send(out_ref.at[:, 3, h:h + q], out_ref.at[:, 2, h:h + q], 1, 0),
         send(out_ref.at[:, 1, h + q:rows], out_ref.at[:, 2, h + q:rows], 3, 0),
+        send(tgt.at[3, :, 0], tgt.at[2, :, 0], 0, 1),
+        send(tgt.at[:, 3, 1], tgt.at[:, 2, 1], 1, 0),
     ]
     phase((1, 3))
     finish(fourth)
     phase((2,))
 
 
-def gather_and_stats(piece, head_t, sel, n_tp):
+def gather_and_stats(piece, head_t, tin, n_tp):
     rows, cols = piece.shape
     vdev = head_t.shape[0]
     h = rows // 2
@@ -175,18 +189,19 @@
         in_specs=[pl.BlockSpec(memory_space=pl.ANY)] * 3,
         out_specs=(pl.BlockSpec(memory_space=pl.ANY), pl.BlockSpec(memory_space=pltpu.VMEM)),
         scratch_shapes=[
-            pltpu.VMEM((2 * vdev + sel.shape[0], cols), jnp.bfloat16),
+            pltpu.VMEM((2 * vdev, cols), jnp.bfloat16),
             pltpu.VMEM((4, h, cols), jnp.bfloat16),
+            pltpu.VMEM((4, 4, 2, 8, h), jnp.float32),
             pltpu.SemaphoreType.DMA((3,)),
             pltpu.SemaphoreType.DMA((2,)),
-            pltpu.SemaphoreType.DMA((16,)),
-            pltpu.SemaphoreType.DMA((16,)),
+            pltpu.SemaphoreType.DMA((28,)),
+            pltpu.SemaphoreType.DMA((28,)),
             pltpu.SemaphoreType.DMA((4,)),
         ],
         compiler_params=pltpu.CompilerParams(
             collective_id=1, has_side_effects=True, vmem_limit_bytes=60 * 1024 * 1024
         ),
-    )(piece, head_t, sel)
+    )(piece, head_t, tin)
 
 
 def plane_kernel(stats_ref, out_ref, own_sem, send_sems, recv_sems):
@@ -290,12 +305,10 @@
     tp = lax.axis_index("tp")
     n_z = lax.axis_size("z")
     chip = xi * n_z + zi
-    digits = jnp.stack([target_ids % 64, (target_ids // 64) % 64, target_ids // 4096], axis=1)
-    tail = jnp.zeros((rows, EXTRA), jnp.bfloat16).at[:, :3].set(digits.astype(jnp.bfloat16))
-    piece = jnp.concatenate([normed, tail], axis=1)
-    head_t = jnp.concatenate([head, jnp.zeros((EXTRA, vdev), head.dtype)], axis=0).T
-    sel = jnp.zeros((8, dim + EXTRA), jnp.bfloat16).at[jnp.arange(3), dim + jnp.arange(3)].set(1.0)
-    _, stats = gather_and_stats(piece, head_t, sel, n_tp)
+    piece = normed
+    head_t = head.T
+    tin = jnp.broadcast_to(target_ids.astype(jnp.float32).reshape(2, 1, rows // 2), (2, 8, rows // 2))
+    _, stats = gather_and_stats(piece, head_t, tin, n_tp)
     h = rows // 2
     order = jnp.array([0, 3, 2, 1])
     st = stats[:, :4].reshape(4, 2, 4, 4, h)

time: 166 us -> 154 us (0.928)
  Pallas kernels: 143 us -> 137 us
  other arithmetic: 10.7 us -> 6.1 us
    pallas_call x1, Pallas kernels: 128 us -> 122 us  [gather_and_stats(): pl.pallas_call(functools.partial(fused_kernel, n_tp), out_shape=(jax.Shap...]
    another operation x4 -> x0, other arithmetic: 2 us -> none
    transpose x1 -> x0, local copies, waits for them, and re-layouts: 1.99 us -> none  [per_device(): jnp.concatenate([head, jnp.zeros((EXTRA, vdev), head.dtype)], axis=0)]
    unnamed x5 -> x9, local copies, waits for them, and re-layouts: 3.79 us -> 4.88 us
where the time goes in v4:
time: 154 us
  Pallas kernels  137 us (89%)
  local copies, waits for them, and re-layouts  7.63 us (5%)
  other arithmetic  6.1 us (4%)
  between operations  3.23 us (2%)
    pallas_call x1, Pallas kernels, gather_and_stats(): pl.pallas_call(functools.partial(fused_kernel, n_tp), out_shape=(jax.Shap...  122 us
    pallas_call x1, Pallas kernels, exchange_plane(): pl.pallas_call(plane_kernel, out_shape=jax.ShapeDtypeStruct(stats.shape,...  8.46 us
    pallas_call x1, Pallas kernels, exchange_tp(): pl.pallas_call(tp_kernel, out_shape=jax.ShapeDtypeStruct((n_tp, *own.shap...  6.52 us
    unnamed x9, local copies, waits for them, and re-layouts  4.88 us

profile of v4, /device:TPU:0, one launch (start us, length us, event | category | flops | bytes accessed | tf_op | source)
XLA Modules:
  0.0 153.7 jit_solution(3334664458231825179)
XLA Ops:
  0.6 0.0 copy-start
  0.6 0.0 copy-start.1
  0.7 4.9 %copy.15 = bf16[2048,768]{0,1:T(8,128)(2,1)} copy(bf16[2048,768]{1,0:T(8,128)(2,1)} %param.8) | data formatting | bytes 6291456 | tf_op args[2]
  5.5 0.0 copy-start.2
  5.5 0.0 copy-done
  5.5 0.3 fusion
  5.8 0.0 copy-done.1
  5.8 1.3 fusion.2.piece_ref
  7.1 0.0 copy-done.2
  7.1 0.6 broadcast_in_dim.24.tin_ref
  7.7 0.0 copy-start.3
  7.7 121.8 %shard_map.93 = (bf16[4,4,256,2048]{3,2,1,0:T(8,128)(2,1)}, f32[8,8,512]{2,1,0:T(8,128)}) custom-call(bf16[256,2048]{1,0:T(8,128)(2,1)} %fusion.2.piece_ref, bf16[768,2048]{1,0:T(8,128)(2,1)} %bitcast.69, f32[2,8,128]{2,1,0:T(8,128)} %broadcast_in_dim.24.tin_ref), custom_call_target="tpu_custom_call" | custom-call | tf_op jit(solution)/shard_map/pallas_call | solution.py:183
  129.5 0.9 slice.35
  130.5 0.0 copy-done.3
  130.5 0.6 gather_fusion.1
  131.1 0.6 gather_fusion
  131.7 0.6 maximum_bitcast_fusion.stats_ref
  132.4 8.5 %shard_map.94 = f32[4,4,4,256]{3,2,1,0:T(4,128)} custom-call(f32[4,4,4,256]{3,2,1,0:T(4,128)} %maximum_bitcast_fusion.stats_ref), custom_call_target="tpu_custom_call" | custom-call | tf_op jit(solution)/shard_map/pallas_call | solution.py:237
  140.8 1.1 fusion.14
  141.9 0.6 pad_maximum_fusion.own_ref
  142.5 6.5 %shard_map.95 = f32[4,4,256]{2,1,0:T(4,128)} custom-call(f32[4,256]{1,0:T(4,128)} %pad_maximum_fusion.own_ref), custom_call_target="tpu_custom_call" | custom-call | tf_op jit(solution)/shard_map/pallas_call | solution.py:281
  149.1 0.9 fusion.16
  150.6 1.3 fusion.13
  (10 shorter events, 0.1 us)
Async XLA Ops:
  0.6 4.9 %copy-start = (bf16[256,2048]{1,0:T(8,128)(2,1)S(1)}, bf16[256,2048]{1,0:T(8,128)(2,1)}, u32[]{:S(2)}) copy-start(bf16[256,2048]{1,0:T(8,128)(2,1)} %param.6) | copy-start | bytes 3145732
  0.6 5.2 %copy-start.1 = (f32[2048]{0:T(1024)S(1)}, f32[2048]{0:T(1024)}, u32[]{:S(2)}) copy-start(f32[2048]{0:T(1024)} %param.7) | copy-start | bytes 24580
  5.5 1.6 %copy-start.2 = (s32[256]{0:T(256)S(1)}, s32[256]{0:T(256)}, u32[]{:S(2)}) copy-start(s32[256]{0:T(256)} %param.9) | copy-start | bytes 3076
  7.7 122.8 %copy-start.3 = (s32[4]{0:T(128)S(1)}, s32[4]{0:T(128)}, u32[]{:S(2)}) copy-start(s32[4]{0:T(128)} %constant.23) | copy-start | bytes 52

commit v5 on v4

--- a/solution.py
+++ b/solution.py
@@ -204,26 +204,28 @@
     )(piece, head_t, tin)
 
 
-def plane_kernel(stats_ref, out_ref, own_sem, send_sems, recv_sems):
+def plane_kernel(n_tp, stats_ref, out_ref, own_sem, send_sems, recv_sems):
     xi, zi = lax.axis_index("x"), lax.axis_index("z")
     core, tp = lax.axis_index("core"), lax.axis_index("tp")
-    offsets = [(dx, dz) for dz in range(4) for dx in range(4) if dx or dz]
+    offsets = [(dx, dz, dy) for dy in range(n_tp) for dz in range(4) for dx in range(4) if dx or dz or dy]
+
+    def peer(dx, dz, dy):
+        return (lax.rem(xi + dx, 4), lax.rem(zi + dz, 4), core, lax.rem(tp + dy, n_tp))
+
     barrier = pltpu.get_barrier_semaphore()
-    for dx, dz in offsets:
-        peer = (lax.rem(xi + dx, 4), lax.rem(zi + dz, 4), core, tp)
-        pl.semaphore_signal(barrier, inc=1, device_id=peer, device_id_type=MESH)
+    for dx, dz, dy in offsets:
+        pl.semaphore_signal(barrier, inc=1, device_id=peer(dx, dz, dy), device_id_type=MESH)
     pl.semaphore_wait(barrier, len(offsets))
-    own = pltpu.make_async_copy(stats_ref.at[0, 0], out_ref.at[0, 0], own_sem)
+    own = pltpu.make_async_copy(stats_ref.at[0, 0], out_ref.at[0, 0, 0], own_sem)
     own.start()
     cps = []
-    for k, (dx, dz) in enumerate(offsets):
-        peer = (lax.rem(xi + dx, 4), lax.rem(zi + dz, 4), core, tp)
+    for k, (dx, dz, dy) in enumerate(offsets):
         cp = pltpu.make_async_remote_copy(
             src_ref=stats_ref.at[dz, dx],
-            dst_ref=out_ref.at[(4 - dz) % 4, (4 - dx) % 4],
+            dst_ref=out_ref.at[(n_tp - dy) % n_tp, (4 - dz) % 4, (4 - dx) % 4],
             send_sem=send_sems.at[k],
             recv_sem=recv_sems.at[k],
-            device_id=peer,
+            device_id=peer(dx, dz, dy),
             device_id_type=MESH,
         )
         cp.start()
@@ -233,63 +235,20 @@
         cp.wait()
 
 
-def exchange_plane(stats):
+def exchange_all(stats, n_tp):
+    n = n_tp * 16 - 1
     return pl.pallas_call(
-        plane_kernel,
-        out_shape=jax.ShapeDtypeStruct(stats.shape, stats.dtype),
+        functools.partial(plane_kernel, n_tp),
+        out_shape=jax.ShapeDtypeStruct((n_tp, *stats.shape), stats.dtype),
         in_specs=[pl.BlockSpec(memory_space=pl.ANY)],
         out_specs=pl.BlockSpec(memory_space=pl.ANY),
         scratch_shapes=[
             pltpu.SemaphoreType.DMA,
-            pltpu.SemaphoreType.DMA((15,)),
-            pltpu.SemaphoreType.DMA((15,)),
+            pltpu.SemaphoreType.DMA((n,)),
+            pltpu.SemaphoreType.DMA((n,)),
         ],
         compiler_params=pltpu.CompilerParams(collective_id=2, has_side_effects=True),
     )(stats)
-
-
-def tp_kernel(own_ref, out_ref, own_sem, send_sems, recv_sems):
-    xi, zi = lax.axis_index("x"), lax.axis_index("z")
-    core, tp = lax.axis_index("core"), lax.axis_index("tp")
-    n = out_ref.shape[0]
-    barrier = pltpu.get_barrier_semaphore()
-    for d in range(1, n):
-        peer = (xi, zi, core, lax.rem(tp + d, n))
-        pl.semaphore_signal(barrier, inc=1, device_id=peer, device_id_type=MESH)
-    pl.semaphore_wait(barrier, n - 1)
-    own = pltpu.make_async_copy(own_ref, out_ref.at[tp], own_sem)
-    own.start()
-    cps = []
-    for d in range(1, n):
-        peer = (xi, zi, core, lax.rem(tp + d, n))
-        cp = pltpu.make_async_remote_copy(
-            src_ref=own_ref,
-            dst_ref=out_ref.at[tp],
-            send_sem=send_sems.at[d - 1],
-            recv_sem=recv_sems.at[d - 1],
-            device_id=peer,
-            device_id_type=MESH,
-        )
-        cp.start()
-        cps.append(cp)
-    own.wait()
-    for cp in cps:
-        cp.wait()
-
-
-def exchange_tp(own, n_tp):
-    return pl.pallas_call(
-        tp_kernel,
-        out_shape=jax.ShapeDtypeStruct((n_tp, *own.shape), own.dtype),
-        in_specs=[pl.BlockSpec(memory_space=pl.ANY)],
-        out_specs=pl.BlockSpec(memory_space=pl.ANY),
-        scratch_shapes=[
-            pltpu.SemaphoreType.DMA,
-            pltpu.SemaphoreType.DMA((n_tp - 1,)),
-            pltpu.SemaphoreType.DMA((n_tp - 1,)),
-        ],
-        compiler_params=pltpu.CompilerParams(collective_id=3, has_side_effects=True),
-    )(own)
 
 
 def per_device(hidden_states, norm_gain, head, target_ids, lengths):
@@ -315,10 +274,9 @@
     s_a = jnp.transpose(st[:, 0], (1, 0, 2, 3))[:, order]
     s_b = jnp.transpose(st[:, 1], (1, 2, 0, 3))[:, :, order]
     rel = jnp.concatenate([s_a, s_b], axis=3)
-    arrived = exchange_plane(jnp.moveaxis(rel, 0, 2))
-    own = jnp.stack(merge(arrived.reshape(16, 4, rows), axis=0))
-    everyone = exchange_tp(own, n_tp)
-    top, weight_sum, weighted, picked = merge(everyone, axis=0)
+    arrived = exchange_all(jnp.moveaxis(rel, 0, 2), n_tp)
+    arrived = jnp.roll(arrived, tp, axis=0)
+    top, weight_sum, weighted, picked = merge(arrived.reshape(-1, 4, rows), axis=0)
     log_norm = top + jnp.log(weight_sum)
     live = jnp.arange(rows, dtype=jnp.int32) < lengths[0]
     logprob = jnp.where(live, picked - log_norm, jnp.float32(0.0))

time: 154 us -> 152 us (0.987)
    pallas_call x2 -> x1, Pallas kernels: 15 us -> 13.8 us  [exchange_all(): pl.pallas_call(functools.partial(plane_kernel, n_tp), out_shape=jax.Shape...]
where the time goes in v5:
time: 152 us; the launch traced here: 151 us
  Pallas kernels  136 us (89%)
  local copies, waits for them, and re-layouts  7.63 us (5%)
  other arithmetic  4.83 us (3%)
  between operations  3.24 us (2%)
    pallas_call x1, Pallas kernels, gather_and_stats(): pl.pallas_call(functools.partial(fused_kernel, n_tp), out_shape=(jax.Shap...  122 us
    pallas_call x1, Pallas kernels, exchange_all(): pl.pallas_call(functools.partial(plane_kernel, n_tp), out_shape=jax.Shape...  13.8 us
    unnamed x9, local copies, waits for them, and re-layouts  4.88 us

profile of v5, /device:TPU:0, one launch (start us, length us, event | category | flops | bytes accessed | tf_op | source)
XLA Modules:
  0.0 151.3 jit_solution(15655994027085756625)
XLA Ops:
  0.6 0.0 copy-start
  0.7 0.0 copy-start.1
  0.7 4.9 %copy.13 = bf16[2048,768]{0,1:T(8,128)(2,1)} copy(bf16[2048,768]{1,0:T(8,128)(2,1)} %param.8) | data formatting | bytes 6291456 | tf_op args[2]
  5.5 0.0 copy-start.2
  5.5 0.0 copy-done
  5.5 0.3 fusion
  5.8 0.0 copy-done.1
  5.8 1.3 fusion.2.piece_ref
  7.1 0.0 copy-done.2
  7.1 0.6 broadcast_in_dim.23.tin_ref
  7.7 0.0 copy-start.3
  7.7 121.8 %shard_map.93 = (bf16[4,4,256,2048]{3,2,1,0:T(8,128)(2,1)}, f32[8,8,512]{2,1,0:T(8,128)}) custom-call(bf16[256,2048]{1,0:T(8,128)(2,1)} %fusion.2.piece_ref, bf16[768,2048]{1,0:T(8,128)(2,1)} %bitcast.45, f32[2,8,128]{2,1,0:T(8,128)} %broadcast_in_dim.23.tin_ref), custom_call_target="tpu_custom_call" | custom-call | tf_op jit(solution)/shard_map/pallas_call | solution.py:183
  129.5 0.9 slice.22
  130.5 0.0 copy-done.3
  130.5 0.6 gather_fusion.1
  131.1 0.6 gather_fusion
  131.7 0.6 maximum_bitcast_fusion.stats_ref
  132.4 13.8 %shard_map.94 = f32[4,4,4,4,256]{4,3,2,1,0:T(4,128)} custom-call(f32[4,4,4,256]{3,2,1,0:T(4,128)} %maximum_bitcast_fusion.stats_ref), custom_call_target="tpu_custom_call" | custom-call | tf_op jit(solution)/shard_map/pallas_call | solution.py:240
  146.2 1.1 fusion.3
  147.3 0.2 fusion.10
  148.2 1.3 fusion.9
  (9 shorter events, 0.1 us)
Async XLA Ops:
  0.6 4.9 %copy-start = (bf16[256,2048]{1,0:T(8,128)(2,1)S(1)}, bf16[256,2048]{1,0:T(8,128)(2,1)}, u32[]{:S(2)}) copy-start(bf16[256,2048]{1,0:T(8,128)(2,1)} %param.6) | copy-start | bytes 3145732
  0.7 5.2 %copy-start.1 = (f32[2048]{0:T(1024)S(1)}, f32[2048]{0:T(1024)}, u32[]{:S(2)}) copy-start(f32[2048]{0:T(1024)} %param.7) | copy-start | bytes 24580
  5.5 1.6 %copy-start.2 = (s32[256]{0:T(256)S(1)}, s32[256]{0:T(256)}, u32[]{:S(2)}) copy-start(s32[256]{0:T(256)} %param.9) | copy-start | bytes 3076
  7.7 122.8 %copy-start.3 = (s32[4]{0:T(128)S(1)}, s32[4]{0:T(128)}, u32[]{:S(2)}) copy-start(s32[4]{0:T(128)} %constant.47) | copy-start | bytes 52

commit v6 on v5

--- a/solution.py
+++ b/solution.py
@@ -35,10 +35,10 @@
 
 
 def fused_kernel(n_tp, piece_ref, head_ref, tin_ref, out_ref, stats_ref,
-                 hboth, vbuf, tgt, local_sems, head_sems, send_sems, recv_sems, load_sems):
+                 hboth, raw, vbuf, tgt, local_sems, head_sems, send_sems, recv_sems, load_sems):
     xi, zi = lax.axis_index("x"), lax.axis_index("z")
     core, tp = lax.axis_index("core"), lax.axis_index("tp")
-    vdev = head_ref.shape[0]
+    vdev = head_ref.shape[1]
 
     def dev(dx, dz):
         return (lax.rem(xi + dx, 4), lax.rem(zi + dz, 4), core, tp)
@@ -50,16 +50,17 @@
     pl.semaphore_signal(barrier, inc=1, device_id=partner, device_id_type=MESH)
     pl.semaphore_wait(barrier, 5)
     mine = pl.ds(pl.multiple_of(core * vdev, vdev), vdev)
+    theirs = pl.ds(pl.multiple_of((1 - core) * vdev, vdev), vdev)
     swap = pltpu.make_async_remote_copy(
         src_ref=head_ref,
-        dst_ref=hboth.at[mine],
+        dst_ref=raw.at[1],
         send_sem=head_sems.at[0],
         recv_sem=head_sems.at[1],
         device_id=partner,
         device_id_type=MESH,
     )
     swap.start()
-    own_head = pltpu.make_async_copy(head_ref, hboth.at[mine], local_sems.at[0])
+    own_head = pltpu.make_async_copy(head_ref, raw.at[0], local_sems.at[0])
     own_head.start()
     sel = pltpu.make_async_copy(tin_ref, tgt.at[0, 0], local_sems.at[1])
     sel.start()
@@ -129,7 +130,7 @@
 
         lax.fori_loop(0, len(ms), body, 0)
 
-    finish([
+    first = [
         send(piece_ref.at[0:h], out_ref.at[0, 3, 0:h], 1, 0),
         send(piece_ref.at[0:h], out_ref.at[0, 1, 0:h], 3, 0),
         send(piece_ref.at[h:rows], out_ref.at[3, 0, h:rows], 0, 1),
@@ -138,15 +139,21 @@
         send(tin_ref.at[0], tgt.at[0, 1, 0], 3, 0),
         send(tin_ref.at[1], tgt.at[3, 0, 1], 0, 1),
         send(tin_ref.at[1], tgt.at[1, 0, 1], 0, 3),
-    ])
-    finish([
+    ]
+    own_head.wait()
+    hboth[mine] = raw[0].T
+    finish(first)
+    second = [
         send(out_ref.at[0, 3, 0:q], out_ref.at[0, 2, 0:q], 1, 0),
         send(out_ref.at[0, 1, q:h], out_ref.at[0, 2, q:h], 3, 0),
         send(out_ref.at[3, 0, h:h + q], out_ref.at[2, 0, h:h + q], 0, 1),
         send(out_ref.at[1, 0, h + q:rows], out_ref.at[2, 0, h + q:rows], 0, 3),
         send(tgt.at[0, 3, 0], tgt.at[0, 2, 0], 1, 0),
         send(tgt.at[3, 0, 1], tgt.at[2, 0, 1], 0, 1),
-    ])
+    ]
+    swap.wait()
+    hboth[theirs] = raw[1].T
+    finish(second)
     own.wait()
     sel.wait()
     third = [
@@ -159,8 +166,6 @@
         send(tgt.at[:, 0, 1], tgt.at[:, 3, 1], 1, 0),
         send(tgt.at[:, 0, 1], tgt.at[:, 1, 1], 3, 0),
     ]
-    swap.wait()
-    own_head.wait()
     phase((0,))
     finish(third)
     fourth = [
@@ -178,7 +183,7 @@
 
 def gather_and_stats(piece, head_t, tin, n_tp):
     rows, cols = piece.shape
-    vdev = head_t.shape[0]
+    vdev = head_t.shape[1]
     h = rows // 2
     return pl.pallas_call(
         functools.partial(fused_kernel, n_tp),
@@ -190,6 +195,7 @@
         out_specs=(pl.BlockSpec(memory_space=pl.ANY), pl.BlockSpec(memory_space=pltpu.VMEM)),
         scratch_shapes=[
             pltpu.VMEM((2 * vdev, cols), jnp.bfloat16),
+            pltpu.VMEM((2, cols, vdev), jnp.bfloat16),
             pltpu.VMEM((4, h, cols), jnp.bfloat16),
             pltpu.VMEM((4, 4, 2, 8, h), jnp.float32),
             pltpu.SemaphoreType.DMA((3,)),
@@ -265,7 +271,7 @@
     n_z = lax.axis_size("z")
     chip = xi * n_z + zi
     piece = normed
-    head_t = head.T
+    head_t = head
     tin = jnp.broadcast_to(target_ids.astype(jnp.float32).reshape(2, 1, rows // 2), (2, 8, rows // 2))
     _, stats = gather_and_stats(piece, head_t, tin, n_tp)
     h = rows // 2

time: 152 us -> 149 us (0.980)
  local copies, waits for them, and re-layouts: 7.63 us -> 2.76 us
  other arithmetic: 4.83 us -> 7.29 us
    unnamed x9 -> x4, local copies, waits for them, and re-layouts: 4.88 us -> 0.01 us
where the time goes in v6:
time: 149 us
  Pallas kernels  136 us (91%)
  other arithmetic  7.29 us (5%)
  between operations  3.22 us (2%)
  local copies, waits for them, and re-layouts  2.76 us (2%)
    pallas_call x1, Pallas kernels, gather_and_stats(): pl.pallas_call(functools.partial(fused_kernel, n_tp), out_shape=(jax.Shap...  122 us
    pallas_call x1, Pallas kernels, exchange_all(): pl.pallas_call(functools.partial(plane_kernel, n_tp), out_shape=jax.Shape...  13.8 us

profile of v6, /device:TPU:0, one launch (start us, length us, event | category | flops | bytes accessed | tf_op | source)
XLA Modules:
  0.0 148.9 jit_solution(6063488746910206983)
XLA Ops:
  0.6 0.0 copy-start
  0.7 1.5 %fusion = f32[256]{0:T(256)S(1)} fusion(bf16[256,2048]{1,0:T(8,128)(2,1)} %param.6), kind=kLoop, calls=%fused_computation.4 | loop fusion | flops 1572608 | bytes 1049600 | tf_op jit(solution)/shard_map/reduce_sum | solution.py:262
  2.2 2.5 %fusion.2.piece_ref = bf16[256,2048]{1,0:T(8,128)(2,1)} fusion(bf16[256,2048]{1,0:T(8,128)(2,1)} %param.6, f32[2048]{0:T(1024)} %param.7, f32[256]{0:T(256)S(1)} %add_rsqrt_fusion), kind=kLoop, calls=%fused_computation.6 | loop fusion | flops 2097152 | bytes 2106368 | tf_op jit(solution)/shard_map/convert_element_type | solution.py:263
  4.7 0.0 copy-done
  4.7 0.6 broadcast_in_dim.23.tin_ref
  5.3 0.0 copy-start.1
  5.3 121.8 %shard_map.93 = (bf16[4,4,256,2048]{3,2,1,0:T(8,128)(2,1)}, f32[8,8,512]{2,1,0:T(8,128)}) custom-call(bf16[256,2048]{1,0:T(8,128)(2,1)} %fusion.2.piece_ref, bf16[2048,768]{1,0:T(8,128)(2,1)} %head_ref.1, f32[2,8,128]{2,1,0:T(8,128)} %broadcast_in_dim.23.tin_ref), custom_call_target="tpu_custom_call" | custom-call | tf_op jit(solution)/shard_map/pallas_call | solution.py:188
  127.1 0.9 slice.22
  128.1 0.0 copy-done.1
  128.1 0.6 gather_fusion.1
  128.7 0.6 gather_fusion
  129.3 0.6 maximum_bitcast_fusion.stats_ref
  130.0 13.8 %shard_map.94 = f32[4,4,4,4,256]{4,3,2,1,0:T(4,128)} custom-call(f32[4,4,4,256]{3,2,1,0:T(4,128)} %maximum_bitcast_fusion.stats_ref), custom_call_target="tpu_custom_call" | custom-call | tf_op jit(solution)/shard_map/pallas_call | solution.py:246
  143.8 1.1 fusion.3
  144.9 0.2 fusion.10
  145.8 1.3 fusion.9
  (9 shorter events, 0.1 us)
Async XLA Ops:
  0.6 4.1 %copy-start = (s32[256]{0:T(256)S(1)}, s32[256]{0:T(256)}, u32[]{:S(2)}) copy-start(s32[256]{0:T(256)} %param.9) | copy-start | bytes 3076
  5.3 122.8 %copy-start.1 = (s32[4]{0:T(128)S(1)}, s32[4]{0:T(128)}, u32[]{:S(2)}) copy-start(s32[4]{0:T(128)} %constant.47) | copy-start | bytes 52

commit v7 on v6

--- a/solution.py
+++ b/solution.py
@@ -275,10 +275,10 @@
     tin = jnp.broadcast_to(target_ids.astype(jnp.float32).reshape(2, 1, rows // 2), (2, 8, rows // 2))
     _, stats = gather_and_stats(piece, head_t, tin, n_tp)
     h = rows // 2
-    order = jnp.array([0, 3, 2, 1])
     st = stats[:, :4].reshape(4, 2, 4, 4, h)
-    s_a = jnp.transpose(st[:, 0], (1, 0, 2, 3))[:, order]
-    s_b = jnp.transpose(st[:, 1], (1, 2, 0, 3))[:, :, order]
+    by_offset = jnp.stack([st[0], st[3], st[2], st[1]])
+    s_a = jnp.transpose(by_offset[:, 0], (1, 0, 2, 3))
+    s_b = jnp.transpose(by_offset[:, 1], (1, 2, 0, 3))
     rel = jnp.concatenate([s_a, s_b], axis=3)
     arrived = exchange_all(jnp.moveaxis(rel, 0, 2), n_tp)
     arrived = jnp.roll(arrived, tp, axis=0)

time: 149 us -> 148 us (level)
  no operation moved by 1% of the time
where the time goes in v7:
time: 148 us
  Pallas kernels  136 us (92%)
  other arithmetic  7.31 us (5%)
  between operations  3.18 us (2%)
    pallas_call x1, Pallas kernels, gather_and_stats(): pl.pallas_call(functools.partial(fused_kernel, n_tp), out_shape=(jax.Shap...  122 us
    pallas_call x1, Pallas kernels, exchange_all(): pl.pallas_call(functools.partial(plane_kernel, n_tp), out_shape=jax.Shape...  13.8 us

profile of v7, /device:TPU:0, one launch (start us, length us, event | category | flops | bytes accessed | tf_op | source)
XLA Modules:
  0.0 147.5 jit_solution(10985047640886784209)
XLA Ops:
  0.6 0.0 copy-start
  0.7 1.5 %fusion = f32[256]{0:T(256)S(1)} fusion(bf16[256,2048]{1,0:T(8,128)(2,1)} %param.5), kind=kLoop, calls=%fused_computation.2 | loop fusion | flops 1572608 | bytes 1049600 | tf_op jit(solution)/shard_map/reduce_sum | solution.py:262
  2.2 2.5 %fusion.2.piece_ref = bf16[256,2048]{1,0:T(8,128)(2,1)} fusion(bf16[256,2048]{1,0:T(8,128)(2,1)} %param.5, f32[2048]{0:T(1024)} %param.6, f32[256]{0:T(256)S(1)} %add_rsqrt_fusion), kind=kLoop, calls=%fused_computation.4 | loop fusion | flops 2097152 | bytes 2106368 | tf_op jit(solution)/shard_map/convert_element_type | solution.py:263
  4.7 0.0 copy-done
  4.7 0.6 broadcast_in_dim.19.tin_ref
  5.3 121.8 %shard_map.84 = (bf16[4,4,256,2048]{3,2,1,0:T(8,128)(2,1)}, f32[8,8,512]{2,1,0:T(8,128)}) custom-call(bf16[256,2048]{1,0:T(8,128)(2,1)} %fusion.2.piece_ref, bf16[2048,768]{1,0:T(8,128)(2,1)} %head_ref.1, f32[2,8,128]{2,1,0:T(8,128)} %broadcast_in_dim.19.tin_ref), custom_call_target="tpu_custom_call" | custom-call | tf_op jit(solution)/shard_map/pallas_call | solution.py:188
  127.1 0.8 slice_bitcast_fusion.5
  128.0 0.6 maximum_bitcast_fusion.stats_ref
  128.6 13.8 %shard_map.85 = f32[4,4,4,4,256]{4,3,2,1,0:T(4,128)} custom-call(f32[4,4,4,256]{3,2,1,0:T(4,128)} %maximum_bitcast_fusion.stats_ref), custom_call_target="tpu_custom_call" | custom-call | tf_op jit(solution)/shard_map/pallas_call | solution.py:246
  142.5 1.1 fusion.3
  143.5 0.2 fusion.10
  144.5 1.3 fusion.9
  (5 shorter events, 0.1 us)
Async XLA Ops:
  0.6 4.1 %copy-start = (s32[256]{0:T(256)S(1)}, s32[256]{0:T(256)}, u32[]{:S(2)}) copy-start(s32[256]{0:T(256)} %param.8) | copy-start | bytes 3076

commit v8 on v7

--- a/solution.py
+++ b/solution.py
@@ -189,7 +189,7 @@
         functools.partial(fused_kernel, n_tp),
         out_shape=(
             jax.ShapeDtypeStruct((4, 4, rows, cols), piece.dtype),
-            jax.ShapeDtypeStruct((8, 8, 4 * h), jnp.float32),
+            jax.ShapeDtypeStruct((8, 4, 4 * h), jnp.float32),
         ),
         in_specs=[pl.BlockSpec(memory_space=pl.ANY)] * 3,
         out_specs=(pl.BlockSpec(memory_space=pl.ANY), pl.BlockSpec(memory_space=pltpu.VMEM)),
@@ -275,7 +275,7 @@
     tin = jnp.broadcast_to(target_ids.astype(jnp.float32).reshape(2, 1, rows // 2), (2, 8, rows // 2))
     _, stats = gather_and_stats(piece, head_t, tin, n_tp)
     h = rows // 2
-    st = stats[:, :4].reshape(4, 2, 4, 4, h)
+    st = stats.reshape(4, 2, 4, 4, h)
     by_offset = jnp.stack([st[0], st[3], st[2], st[1]])
     s_a = jnp.transpose(by_offset[:, 0], (1, 0, 2, 3))
     s_b = jnp.transpose(by_offset[:, 1], (1, 2, 0, 3))

time: 148 us -> 148 us (level)
  no operation moved by 1% of the time
where the time goes in v8:
time: 148 us; the launch traced here: 147 us
  Pallas kernels  136 us (92%)
  other arithmetic  7.3 us (5%)
  between operations  3.17 us (2%)
    pallas_call x1, Pallas kernels, gather_and_stats(): pl.pallas_call(functools.partial(fused_kernel, n_tp), out_shape=(jax.Shap...  122 us
    pallas_call x1, Pallas kernels, exchange_all(): pl.pallas_call(functools.partial(plane_kernel, n_tp), out_shape=jax.Shape...  13.8 us

profile of v8, /device:TPU:0, one launch (start us, length us, event | category | flops | bytes accessed | tf_op | source)
XLA Modules:
  0.0 147.5 jit_solution(1944824305935676095)
XLA Ops:
  0.6 0.0 copy-start
  0.7 1.5 %fusion = f32[256]{0:T(256)S(1)} fusion(bf16[256,2048]{1,0:T(8,128)(2,1)} %param.5), kind=kLoop, calls=%fused_computation.2 | loop fusion | flops 1572608 | bytes 1049600 | tf_op jit(solution)/shard_map/reduce_sum | solution.py:262
  2.2 2.5 %fusion.2.piece_ref = bf16[256,2048]{1,0:T(8,128)(2,1)} fusion(bf16[256,2048]{1,0:T(8,128)(2,1)} %param.5, f32[2048]{0:T(1024)} %param.6, f32[256]{0:T(256)S(1)} %add_rsqrt_fusion), kind=kLoop, calls=%fused_computation.4 | loop fusion | flops 2097152 | bytes 2106368 | tf_op jit(solution)/shard_map/convert_element_type | solution.py:263
  4.7 0.0 copy-done
  4.7 0.6 broadcast_in_dim.19.tin_ref
  5.3 121.8 %shard_map.84 = (bf16[4,4,256,2048]{3,2,1,0:T(8,128)(2,1)}, f32[8,4,512]{2,1,0:T(4,128)}) custom-call(bf16[256,2048]{1,0:T(8,128)(2,1)} %fusion.2.piece_ref, bf16[2048,768]{1,0:T(8,128)(2,1)} %head_ref.1, f32[2,8,128]{2,1,0:T(8,128)} %broadcast_in_dim.19.tin_ref), custom_call_target="tpu_custom_call" | custom-call | tf_op jit(solution)/shard_map/pallas_call | solution.py:188
  127.1 0.8 slice_bitcast_fusion.5
  127.9 0.6 maximum_bitcast_fusion.stats_ref
  128.5 13.8 %shard_map.85 = f32[4,4,4,4,256]{4,3,2,1,0:T(4,128)} custom-call(f32[4,4,4,256]{3,2,1,0:T(4,128)} %maximum_bitcast_fusion.stats_ref), custom_call_target="tpu_custom_call" | custom-call | tf_op jit(solution)/shard_map/pallas_call | solution.py:246
  142.4 1.1 fusion.3
  143.5 0.2 fusion.10
  144.4 1.3 fusion.9
  (5 shorter events, 0.1 us)
Async XLA Ops:
  0.6 4.1 %copy-start = (s32[256]{0:T(256)S(1)}, s32[256]{0:T(256)}, u32[]{:S(2)}) copy-start(s32[256]{0:T(256)} %param.8) | copy-start | bytes 3076

commit v9 on v8

--- a/solution.py
+++ b/solution.py
@@ -257,10 +257,21 @@
     )(stats)
 
 
+def norm_kernel(h_ref, g_ref, o_ref):
+    feats = h_ref[...].astype(jnp.float32)
+    scale = lax.rsqrt(jnp.mean(feats * feats, axis=-1, keepdims=True) + 1e-06)
+    o_ref[...] = (feats * scale * g_ref[...]).astype(jnp.bfloat16)
+
+
+def rms_norm(hidden_states, norm_gain):
+    return pl.pallas_call(
+        norm_kernel,
+        out_shape=jax.ShapeDtypeStruct(hidden_states.shape, jnp.bfloat16),
+    )(hidden_states, norm_gain.reshape(1, -1))
+
+
 def per_device(hidden_states, norm_gain, head, target_ids, lengths):
-    feats = hidden_states.astype(jnp.float32)
-    scale = lax.rsqrt(jnp.mean(feats * feats, axis=-1, keepdims=True) + 1e-06)
-    normed = (feats * scale * norm_gain).astype(jnp.bfloat16)
+    normed = rms_norm(hidden_states, norm_gain)
     rows, dim = normed.shape
     vdev = head.shape[1]
     n_tp = lax.axis_size("tp")

time: 148 us -> 147 us (level)
  other arithmetic: 7.3 us -> 3.93 us
  Pallas kernels: 136 us -> 138 us
    pallas_call x0 -> x1, Pallas kernels: none -> 2.62 us  [rms_norm(): pl.pallas_call(norm_kernel, out_shape=jax.ShapeDtypeStruct(hidden_states....]
    convert_element_type x1 -> x0, other arithmetic: 2.53 us -> none  [per_device(): normed = (feats * scale * norm_gain).astype(jnp.bfloat16)]
    reduce_sum x1 -> x0, other arithmetic: 1.51 us -> none  [per_device(): scale = lax.rsqrt(jnp.mean(feats * feats, axis=-1, keepdims=True) + 1e-06)]
where the time goes in v9:
time: 147 us
  Pallas kernels  138 us (94%)
  other arithmetic  3.93 us (3%)
  between operations  3.16 us (2%)
    pallas_call x1, Pallas kernels, gather_and_stats(): pl.pallas_call(functools.partial(fused_kernel, n_tp), out_shape=(jax.Shap...  122 us
    pallas_call x1, Pallas kernels, exchange_all(): pl.pallas_call(functools.partial(plane_kernel, n_tp), out_shape=jax.Shape...  13.8 us

profile of v9, /device:TPU:0, one launch (start us, length us, event | category | flops | bytes accessed | tf_op | source)
XLA Modules:
  0.0 146.7 jit_solution(13540689143749033274)
XLA Ops:
  0.6 2.6 %shard_map.84.piece_ref = bf16[256,2048]{1,0:T(8,128)(2,1)} custom-call(bf16[256,2048]{1,0:T(8,128)(2,1)} %h_ref.1, f32[1,2048]{1,0:T(1,128)} %bitcast.48), custom_call_target="tpu_custom_call" | custom-call | tf_op jit(solution)/shard_map/pallas_call | solution.py:267
  3.3 0.7 convert_bitcast_fusion
  4.0 0.6 broadcast_in_dim.17.tin_ref
  4.5 121.8 %shard_map.85 = (bf16[4,4,256,2048]{3,2,1,0:T(8,128)(2,1)}, f32[8,4,512]{2,1,0:T(4,128)}) custom-call(bf16[256,2048]{1,0:T(8,128)(2,1)} %shard_map.84.piece_ref, bf16[2048,768]{1,0:T(8,128)(2,1)} %head_ref.1, f32[2,8,128]{2,1,0:T(8,128)} %broadcast_in_dim.17.tin_ref), custom_call_target="tpu_custom_call" | custom-call | tf_op jit(solution)/shard_map/pallas_call | solution.py:188
  126.3 0.8 slice_bitcast_fusion.5
  127.1 0.6 maximum_bitcast_fusion.stats_ref
  127.8 13.8 %shard_map.86 = f32[4,4,4,4,256]{4,3,2,1,0:T(4,128)} custom-call(f32[4,4,4,256]{3,2,1,0:T(4,128)} %maximum_bitcast_fusion.stats_ref), custom_call_target="tpu_custom_call" | custom-call | tf_op jit(solution)/shard_map/pallas_call | solution.py:246
  141.6 1.1 fusion
  142.7 0.2 fusion.7
  143.6 1.3 fusion.6
  (3 shorter events, 0.1 us)

commit v10 on v9

--- a/solution.py
+++ b/solution.py
@@ -112,7 +112,7 @@
             pieces = [tgt[off, j, 0, 0:1, :] for j in range(4)]
         else:
             pieces = [tgt[j, off, 1, 0:1, :] for j in range(4)]
-        target = jnp.concatenate(pieces, axis=1)
+        target = jnp.concatenate(pieces, axis=1).astype(jnp.float32)
         top = jnp.max(real, axis=0, keepdims=True)
         shifted = jnp.exp(real - top)
         g = m * 2 + half
@@ -197,7 +197,7 @@
             pltpu.VMEM((2 * vdev, cols), jnp.bfloat16),
             pltpu.VMEM((2, cols, vdev), jnp.bfloat16),
             pltpu.VMEM((4, h, cols), jnp.bfloat16),
-            pltpu.VMEM((4, 4, 2, 8, h), jnp.float32),
+            pltpu.VMEM((4, 4, 2, 8, h), jnp.int32),
             pltpu.SemaphoreType.DMA((3,)),
             pltpu.SemaphoreType.DMA((2,)),
             pltpu.SemaphoreType.DMA((28,)),
@@ -283,7 +283,7 @@
     chip = xi * n_z + zi
     piece = normed
     head_t = head
-    tin = jnp.broadcast_to(target_ids.astype(jnp.float32).reshape(2, 1, rows // 2), (2, 8, rows // 2))
+    tin = jnp.broadcast_to(target_ids.reshape(2, 1, rows // 2), (2, 8, rows // 2))
     _, stats = gather_and_stats(piece, head_t, tin, n_tp)
     h = rows // 2
     st = stats.reshape(4, 2, 4, 4, h)

time: 147 us -> 147 us (level)
  no operation moved by 1% of the time
where the time goes in v10:
time: 147 us
  Pallas kernels  138 us (94%)
  other arithmetic  3.25 us (2%)
  between operations  3.16 us (2%)
  local copies, waits for them, and re-layouts  2.06 us (1%)
    pallas_call x1, Pallas kernels, gather_and_stats(): pl.pallas_call(functools.partial(fused_kernel, n_tp), out_shape=(jax.Shap...  122 us
    pallas_call x1, Pallas kernels, exchange_all(): pl.pallas_call(functools.partial(plane_kernel, n_tp), out_shape=jax.Shape...  13.8 us

profile of v10, /device:TPU:0, one launch (start us, length us, event | category | flops | bytes accessed | tf_op | source)
XLA Modules:
  0.0 146.6 jit_solution(12040569249034248288)
XLA Ops:
  0.6 2.6 %shard_map.84.piece_ref = bf16[256,2048]{1,0:T(8,128)(2,1)} custom-call(bf16[256,2048]{1,0:T(8,128)(2,1)} %h_ref.1, f32[1,2048]{1,0:T(1,128)} %bitcast.47), custom_call_target="tpu_custom_call" | custom-call | tf_op jit(solution)/shard_map/pallas_call | solution.py:267
  3.3 1.3 broadcast_in_dim.17.tin_ref
  4.5 121.7 %shard_map.85 = (bf16[4,4,256,2048]{3,2,1,0:T(8,128)(2,1)}, f32[8,4,512]{2,1,0:T(4,128)}) custom-call(bf16[256,2048]{1,0:T(8,128)(2,1)} %shard_map.84.piece_ref, bf16[2048,768]{1,0:T(8,128)(2,1)} %head_ref.1, s32[2,8,128]{2,1,0:T(8,128)} %broadcast_in_dim.17.tin_ref), custom_call_target="tpu_custom_call" | custom-call | tf_op jit(solution)/shard_map/pallas_call | solution.py:188
  126.2 0.8 slice_bitcast_fusion.5
  127.0 0.6 maximum_bitcast_fusion.stats_ref
  127.7 13.8 %shard_map.86 = f32[4,4,4,4,256]{4,3,2,1,0:T(4,128)} custom-call(f32[4,4,4,256]{3,2,1,0:T(4,128)} %maximum_bitcast_fusion.stats_ref), custom_call_target="tpu_custom_call" | custom-call | tf_op jit(solution)/shard_map/pallas_call | solution.py:246
  141.5 1.1 fusion
  142.6 0.2 fusion.7
  143.5 1.3 fusion.6
  (3 shorter events, 0.1 us)
